TPU v7x, 256 devices: a whole 4x4x8 slice. The times are simulated.
256 devices in a mesh: tm: 64 (over y, z, core), head: 4 (over x).
Axes of the slice: x: 4, y: 4, z: 8, core: 2. Of those that a mesh axis runs over, the one named last changes fastest.
Arguments:
- series: bfloat16 [16384, 512], P('tm'), may hold values from -16 to 16
- in_weight: bfloat16 [512, 3, 1024], P(None, None, 'head'), may hold values from -0.25 to 0.25
- step_weight: bfloat16 [512, 16], P(None, 'head'), may hold values from -0.25 to 0.25
- step_bias: float32 [16], P('head'), may hold values from -7 to -6
- log_rate: float32 [16], P('head'), as said below
- conv_weight: float32 [4, 2, 1024], P(None, None, 'head'), may hold values from -3 to 3
- conv_bias: float32 [2, 1024], P(None, 'head'), may hold values from -3 to 3
- skip_gain: float32 [16], P('head'), may hold values from 0.5 to 1.5
- norm_gain: float32 [1024], P('head'), may hold values from 0.1 to 1.9
- out_weight: bfloat16 [512, 1024], P(None, 'head'), may hold values from -0.1875 to 0.1875
- cotangent: bfloat16 [16384, 512], P('tm'), may hold values from -6 to 6
Outputs:
- layer_out: bfloat16 [16384, 512], P(('tm', 'head'))
- series_grad: float32 [16384, 512], P(('tm', 'head'))
- w_in_grad: float32 [512, 3, 1024], P('tm', None, 'head')
- w_dt_grad: float32 [512, 16], P('tm', 'head')
- w_out_grad: float32 [512, 1024], P('tm', 'head')
Inputs may be any that keep to these rules, and one draw needn't show every extreme that they name: `log_rate`: each head's logarithm of its decay rate.
All inputs are finite; a program needn't handle non-finite values.
Results may differ from a plain program's by a relative error of at most 0.0076.
Values may be sent and summed in bfloat16 or wider, within the bound.
A program may use at most 64 MiB of HBM per device.

v0:
```python
import jax
import jax.numpy as jnp
from jax import lax
from jax.sharding import PartitionSpec as P

E = 1024
N = 128
KW = 4
BLOCK = 256


NORM_EPSILON = 1e-05
HIGHEST_PRECISION = lax.Precision.HIGHEST
HIGH_PRECISION = lax.Precision.HIGH


def passed_along(block, axis, distance):
    devices = range(lax.axis_size(axis))
    route = [(i - distance, i) for i in devices if i - distance in devices]
    return lax.ppermute(block, axis, route)


def carried_in(x, axis, combine, identity, reverse):
    count, position = (lax.axis_size(axis), lax.axis_index(axis))
    everything = jax.tree.map(lambda part: lax.all_gather(part, axis), x)
    start = jax.tree.map(
        lambda part, zero: jnp.broadcast_to(jnp.asarray(zero, part.dtype), part.shape), x, identity
    )

    def hop(k, before):
        at = count - 1 - k if reverse else k
        reached = at > position if reverse else at < position
        new = combine(before, jax.tree.map(lambda part: part[at], everything))
        return jax.tree.map(lambda a, b: jnp.where(reached, a, b), new, before)

    return lax.fori_loop(0, count, hop, start)


def contract(left_side, right_side, left_dim, right_dim):
    return lax.dot_general(
        left_side,
        right_side,
        (((left_dim,), (right_dim,)), ((), ())),
        preferred_element_type=jnp.float32,
    )


def silu_grad(values):
    sigmoid_v = jax.nn.sigmoid(values)
    return sigmoid_v * (1.0 + values * (1.0 - sigmoid_v))


def decay_table(log_block):
    running = jnp.cumsum(log_block, axis=0)
    length = log_block.shape[0]
    row_ids = lax.broadcasted_iota(jnp.int32, (length, length), 0)
    col_ids = lax.broadcasted_iota(jnp.int32, (length, length), 1)
    log_gap = running.T[:, :, None] - running.T[:, None, :]
    decays = jnp.exp(jnp.where((col_ids <= row_ids)[None], log_gap, -1e30))
    return (running, decays)


def block_forward(x_block, b_block, c_block, step_block, log_block, start_state, skip_gain):
    per_group = x_block.shape[1] // b_block.shape[1]
    x_wide = x_block.astype(jnp.float32)
    b_wide = b_block.astype(jnp.float32)
    c_wide = c_block.astype(jnp.float32)
    b_heads = jnp.repeat(b_wide, per_group, axis=1)
    c_heads = jnp.repeat(c_wide, per_group, axis=1)
    running, decays = decay_table(log_block)
    scores = jnp.einsum("ign,jgn->gij", c_block, b_block, preferred_element_type=jnp.float32)
    mixing = jnp.repeat(scores, per_group, axis=0) * decays * step_block.T[:, None, :]
    inside = jnp.einsum("hij,jhp->ihp", mixing, x_wide, precision=HIGH_PRECISION)
    from_state = jnp.exp(running)[:, :, None] * jnp.einsum(
        "ihn,hpn->ihp", c_heads, start_state, precision=HIGH_PRECISION
    )
    output = inside + from_state + skip_gain[None, :, None] * x_wide
    remain = jnp.exp(running[-1][None, :] - running) * step_block
    end_state = jnp.exp(running[-1])[:, None, None] * start_state + jnp.einsum(
        "jh,jhp,jhn->hpn", remain, x_wide, b_heads, precision=HIGH_PRECISION
    )
    return (output, end_state)


def block_backward(
    x_block,
    b_block,
    c_block,
    step_block,
    log_block,
    start_state,
    skip_gain,
    grad_y,
    ssm_out,
    after_state,
):
    group_count = b_block.shape[1]
    per_group = x_block.shape[1] // group_count
    length = x_block.shape[0]
    x_wide = x_block.astype(jnp.float32)
    b_wide = b_block.astype(jnp.float32)
    c_wide = c_block.astype(jnp.float32)
    b_heads = jnp.repeat(b_wide, per_group, axis=1)
    c_heads = jnp.repeat(c_wide, per_group, axis=1)
    running, decays = decay_table(log_block)
    scores = jnp.einsum("ign,jgn->gij", c_block, b_block, preferred_element_type=jnp.float32)
    weighted = jnp.repeat(scores, per_group, axis=0) * decays
    remain = jnp.exp(running[-1][None, :] - running)
    back_b = jnp.einsum("hit,ihp->thp", weighted, grad_y, precision=HIGH_PRECISION)
    back_b = back_b + remain[:, :, None] * jnp.einsum(
        "thn,hpn->thp", b_heads, after_state, precision=HIGH_PRECISION
    )
    grad_x = skip_gain[None, :, None] * grad_y + step_block[:, :, None] * back_b
    x_back = jnp.sum(x_wide * back_b, axis=2)
    grad_cum = jnp.sum(grad_y * ssm_out, axis=2) - step_block * x_back
    pair_terms = (
        decays
        * jnp.einsum("ihp,jhp->hij", grad_y, x_wide, precision=HIGH_PRECISION)
        * step_block.T[:, None, :]
    )
    group_terms = pair_terms.reshape(group_count, per_group, length, length).sum(axis=1)
    state_c = jnp.exp(running)[:, :, None] * jnp.einsum(
        "ihp,hpn->ihn", grad_y, start_state, precision=HIGH_PRECISION
    )
    grad_c = jnp.einsum(
        "gij,jgn->ign", group_terms, b_wide, precision=HIGH_PRECISION
    ) + state_c.reshape(length, group_count, per_group, -1).sum(axis=2)
    state_b = (step_block * remain)[:, :, None] * jnp.einsum(
        "jhp,hpn->jhn", x_wide, after_state, precision=HIGH_PRECISION
    )
    grad_b = jnp.einsum(
        "gij,ign->jgn", group_terms, c_wide, precision=HIGH_PRECISION
    ) + state_b.reshape(length, group_count, per_group, -1).sum(axis=2)
    before = jnp.exp(running[-1])[:, None, None] * after_state + jnp.einsum(
        "ih,ihp,ihn->hpn", jnp.exp(running), grad_y, c_heads, precision=HIGH_PRECISION
    )
    return (grad_x, grad_b, grad_c, x_back, grad_cum, before)


def conv_rims(values, shift_by):
    return passed_along(values, "tm", shift_by)


def link_states(earlier_part, later_part):
    return (
        earlier_part[0] + later_part[0],
        jnp.exp(later_part[0])[:, None, None] * earlier_part[1] + later_part[1],
    )


def state_pass(summary, backward):
    identity = (jnp.zeros_like(summary[0]), jnp.zeros_like(summary[1]))
    return carried_in(summary, "tm", link_states, identity, backward)


def channel_total(values):
    return lax.psum(values, "head")


def head_partials(values):
    return lax.psum_scatter(values, "head", scatter_dimension=0, tiled=True)


def body(
    series,
    in_weight,
    step_weight,
    step_bias,
    log_rate,
    conv_weight,
    conv_bias,
    skip_gain,
    norm_gain,
    out_weight,
    cotangent,
):
    row_count = series.shape[0]
    model_width = series.shape[1]
    inner_width = in_weight.shape[2]
    head_count = step_weight.shape[1]
    head_size = inner_width // head_count
    group_count = inner_width // (2 * N)
    per_group = head_count // group_count
    block_count = row_count // BLOCK
    margin = KW - 1
    w_flat = in_weight.reshape(model_width, 3 * inner_width)
    projected = (
        jnp.dot(series, w_flat, preferred_element_type=jnp.float32)
        .astype(jnp.bfloat16)
        .reshape(row_count, 3, inner_width)
    )
    pre_conv = projected[:, 1:, :]
    upper_rim = conv_rims(pre_conv[row_count - margin :].astype(jnp.float32), 1)
    pre_wide = jnp.concatenate([upper_rim, pre_conv.astype(jnp.float32)], axis=0)
    conv_out = conv_bias[None] + conv_weight[0][None] * pre_wide[0:row_count]
    for offset in range(1, KW):
        conv_out = conv_out + conv_weight[offset][None] * pre_wide[offset : offset + row_count]
    activated = jax.nn.silu(conv_out)
    x_heads = activated[:, 0].astype(jnp.bfloat16).reshape(row_count, head_count, head_size)
    bc_values = activated[:, 1].astype(jnp.bfloat16).reshape(row_count, group_count, 2, N)
    b_values = bc_values[:, :, 0]
    c_values = bc_values[:, :, 1]
    gate_raw = projected[:, 0].astype(jnp.float32)
    step_raw = jnp.dot(series, step_weight, preferred_element_type=jnp.float32)
    step_size = jax.nn.softplus(step_raw + step_bias[None])
    decay_rates = jnp.exp(log_rate)
    log_decay = -step_size * decay_rates[None]
    x_wide = x_heads.astype(jnp.float32)
    running = jnp.cumsum(log_decay, axis=0)
    last_log = running[-1]
    own_state = jnp.einsum(
        "lh,lhp,lhn->hpn",
        jnp.exp(last_log[None] - running) * step_size,
        x_wide,
        jnp.repeat(b_values.astype(jnp.float32), per_group, axis=1),
        precision=HIGHEST_PRECISION,
    )
    incoming = state_pass((last_log, own_state), False)[1]
    blocked = (
        x_heads.reshape(block_count, BLOCK, head_count, head_size),
        b_values.reshape(block_count, BLOCK, group_count, N),
        c_values.reshape(block_count, BLOCK, group_count, N),
        step_size.reshape(block_count, BLOCK, head_count),
        log_decay.reshape(block_count, BLOCK, head_count),
    )

    def forward_step(carried, pieces):
        output, end_state = block_forward(
            pieces[0], pieces[1], pieces[2], pieces[3], pieces[4], carried, skip_gain
        )
        return (end_state, (output, carried))

    final_state, (outputs, starts) = lax.scan(forward_step, incoming, blocked)
    y_flat = outputs.reshape(row_count, inner_width)
    gate_act = jax.nn.silu(gate_raw)
    gated_out = y_flat * gate_act
    inv_rms = lax.rsqrt(channel_total(jnp.sum(gated_out * gated_out, axis=1)) / E + NORM_EPSILON)
    normed = (gated_out * inv_rms[:, None] * norm_gain[None]).astype(jnp.bfloat16)
    layer_out = head_partials(contract(normed, out_weight, 1, 1)).astype(jnp.bfloat16)
    grad_normed = jnp.dot(cotangent, out_weight, preferred_element_type=jnp.float32)
    grad_out = contract(cotangent, normed, 0, 0)
    gain_grad = norm_gain[None] * grad_normed
    inner_sum = channel_total(jnp.sum(gated_out * gain_grad, axis=1))
    grad_gated = inv_rms[:, None] * gain_grad - gated_out * (inv_rms**3 * inner_sum / E)[:, None]
    grad_y = (grad_gated * gate_act).reshape(row_count, head_count, head_size)
    grad_gate = grad_gated * y_flat * silu_grad(gate_raw)
    own_back = jnp.einsum(
        "lh,lhp,lhn->hpn",
        jnp.exp(running),
        grad_y,
        jnp.repeat(c_values.astype(jnp.float32), per_group, axis=1),
        precision=HIGHEST_PRECISION,
    )
    after_in = state_pass((last_log, own_back), True)[1]
    ssm_out = outputs - skip_gain[None, None, :, None] * x_wide.reshape(
        block_count, BLOCK, head_count, head_size
    )
    back_inputs = blocked + (
        starts,
        grad_y.reshape(block_count, BLOCK, head_count, head_size),
        ssm_out,
    )

    def backward_step(carried, pieces):
        grad_x, grad_b, grad_c, x_back, grad_cum, before = block_backward(
            pieces[0],
            pieces[1],
            pieces[2],
            pieces[3],
            pieces[4],
            pieces[5],
            skip_gain,
            pieces[6],
            pieces[7],
            carried,
        )
        return (before, (grad_x, grad_b, grad_c, x_back, grad_cum))

    _, (grad_x, grad_b, grad_c, x_back, grad_cum) = lax.scan(
        backward_step, after_in, back_inputs, reverse=True
    )
    grad_cum = grad_cum.reshape(row_count, head_count)
    grad_log = (
        lax.cumsum(grad_cum, axis=0, reverse=True)
        + jnp.sum(after_in * final_state, axis=(1, 2))[None]
    )
    grad_step = x_back.reshape(row_count, head_count) - decay_rates[None] * grad_log
    grad_raw = (grad_step * jax.nn.sigmoid(step_raw + step_bias[None])).astype(jnp.bfloat16)
    grad_bc = jnp.stack(
        [grad_b.reshape(row_count, group_count, N), grad_c.reshape(row_count, group_count, N)],
        axis=2,
    ).reshape(row_count, inner_width)
    grad_act = jnp.stack([grad_x.reshape(row_count, inner_width), grad_bc], axis=1)
    grad_conv = grad_act * silu_grad(conv_out)
    lower_rim = conv_rims(grad_conv[:margin], -1)
    grad_wide = jnp.concatenate([grad_conv, lower_rim], axis=0)
    grad_pre = conv_weight[0][None] * grad_wide[margin : margin + row_count]
    for offset in range(1, KW):
        grad_pre = (
            grad_pre
            + conv_weight[offset][None] * grad_wide[margin - offset : margin - offset + row_count]
        )
    grad_proj = (
        jnp.concatenate([grad_gate[:, None], grad_pre], axis=1)
        .astype(jnp.bfloat16)
        .reshape(row_count, 3 * inner_width)
    )
    grad_in = contract(series, grad_proj, 0, 0).reshape(model_width, 3, inner_width)
    grad_dt = contract(series, grad_raw, 0, 0)
    grad_rows = contract(grad_proj, w_flat, 1, 1) + contract(grad_raw, step_weight, 1, 1)
    series_grad = head_partials(grad_rows)
    w_in_grad, w_dt_grad, w_out_grad = (
        lax.psum_scatter(grad_in, "tm", scatter_dimension=0, tiled=True),
        lax.psum_scatter(grad_dt, "tm", scatter_dimension=0, tiled=True),
        lax.psum_scatter(grad_out, "tm", scatter_dimension=0, tiled=True),
    )
    return (layer_out, series_grad, w_in_grad, w_dt_grad, w_out_grad)


def solution(mesh):
    in_specs = (
        P("tm", None),
        P(None, None, "head"),
        P(None, "head"),
        P("head"),
        P("head"),
        P(None, None, "head"),
        P(None, "head"),
        P("head"),
        P("head"),
        P(None, "head"),
        P("tm", None),
    )
    out_specs = (
        P(("tm", "head"), None),
        P(("tm", "head"), None),
        P("tm", None, "head"),
        P("tm", "head"),
        P("tm", "head"),
    )
    return jax.shard_map(body, mesh=mesh, in_specs=in_specs, out_specs=out_specs, check_vma=False)
```

profile of v0, /device:TPU:1, one launch (start us, length us, event | category | flops | bytes accessed | tf_op | source)
XLA Modules:
  0.0 605.5 jit_solution(17036512634248711002)
XLA Ops:
  7.3 1.5 copy.46
  9.6 4.9 collective-permute-start
  16.1 1.2 reduce-window.24
  19.6 1.0 multiply_convert_fusion
  21.1 1.1 fusion.51
  22.2 41.4 %all-gather.2 = f32[64,1,4]{2,1,0:T(1,128)S(1)} all-gather(f32[1,1,4]{2,1,0:T(1,128)S(1)} %bitcast.287), channel_id=1, replica_groups=mesh['tm'=64,'head'=4] {'tm'}, dimensions={0}, use_global_device_ids=true | all-gather | bytes 1040 | tf_op jit(solution)/shard_map/all_gather | solution.py:25
  63.9 1.4 convolution_bitcast_fusion.7
  65.3 41.9 %all-gather.6.cloned.1.call-done = f32[256,64,128]{2,1,0:T(8,128)} async-done(((f32[4,64,128]{2,1,0:T(8,128)}), f32[256,64,128]{2,1,0:T(8,128)}) %all-gather.6.cloned.1.call-update) | async-done | bytes 8388624 | tf_op jit(solution)/shard_map/all_gather | solution.py:25
  107.3 66.5 %while.20 = (s32[]{:T(128)}, f32[4,64,128]{2,1,0:T(8,128)S(1)}, s32[]{:T(128)}, f32[64,4]{1,0:T(8,128)S(1)}, f32[64,4,64,128]{3,2,1,0:T(8,128)}, /*index=5*/s32[]{:T(128)}, s32[]{:T(128)}) while((s32[]{:T(128)}, f32[4,64,128]{2,1,0:T(8,128)S(1)}, s32[]{:T(128)}, f32[64,4]{1,0:T(8,128)S(1)}, f32[64,4,64,128]{3,2,1,0:T(8,128)}, ...), condition=%wide.region_3.4_spmd.clone, body=%wide.region_2.3_spmd.clone.sunk | while | flops 131076 | bytes 393377 | solution.py:36
  173.8 2.0 multiply_reduce_fusion.1
  176.1 8.5 %all-reduce.1 = (f32[256]{0:T(256)S(1)}, f32[256]{0:T(256)S(1)}) all-reduce(f32[256]{0:T(256)} %get-tuple-element.411, f32[256]{0:T(256)S(1)} %get-tuple-element.386), channel_id=1, replica_groups=mesh['tm'=64,'head'=4] {'head'}, use_global_device_ids=true, to_apply=%region_5.6 | all-reduce | flops 512 | bytes 4096 | tf_op jit(solution)/shard_map/psum | solution.py:157
  184.8 1.1 fusion.63
  185.9 1.1 exp.101
  187.1 1.9 fusion.94
  190.0 1.2 convolution_bitcast_fusion
  191.2 1.1 copy.65
  192.7 1.6 fusion.3
  194.3 1.1 fusion.17
  195.5 2.3 convolution_bitcast_fusion.6
  197.9 67.8 %all-gather.8.cloned.1.call-done = f32[256,64,128]{2,1,0:T(8,128)} async-done(((f32[4,64,128]{2,1,0:T(8,128)}), f32[256,64,128]{2,1,0:T(8,128)}) %all-gather.8.cloned.1.call-update) | async-done | bytes 8388624 | tf_op jit(solution)/shard_map/all_gather | solution.py:25
  265.7 109.6 %while.21 = (s32[]{:T(128)}, f32[4,64,128]{2,1,0:T(8,128)S(1)}, s32[]{:T(128)}, f32[64,4]{1,0:T(8,128)}, f32[64,4,64,128]{3,2,1,0:T(8,128)}, /*index=5*/s32[]{:T(128)}, s32[]{:T(128)}, s32[]{:T(128)}, s32[]{:T(128)}) while((s32[]{:T(128)}, f32[4,64,128]{2,1,0:T(8,128)S(1)}, s32[]{:T(128)}, f32[64,4]{1,0:T(8,128)}, ...), condition=%wide.region_10.11_spmd.clone, body=%wide.region_9.10_spmd.clone.sunk | while | flops 131080 | bytes 393439 | solution.py:36
  316.1 1.0 fusion.127
  322.9 1.0 fusion.127
  376.1 1.4 fusion.54
  377.6 5.0 reduce-window.26
  383.3 2.2 collective-permute-start.1
  386.4 2.2 collective-permute-done.1
  390.1 1.2 convolution_add_fusion
  391.9 1.6 copy.61
  394.8 1.5 convert_element_type.101
  396.5 123.3 %all-reduce = f32[512,4]{0,1:T(4,128)S(1)} all-reduce(f32[512,4]{0,1:T(4,128)S(1)} %convolution_bitcast_fusion.10), channel_id=7, replica_groups=mesh['tm'=64,'head'=4] {'tm'}, use_global_device_ids=true, to_apply=%region_21.22.clone | all-reduce | flops 2048 | bytes 16384
  520.6 78.1 %reduce-scatter.12.cloned.1.call-done = f32[8,3,256]{2,0,1:T(8,128)} async-done(((f32[512,3,256]{2,0,1:T(8,128)}), f32[8,3,256]{2,0,1:T(8,128)}) %reduce-scatter.12.cloned.1.call-update) | async-done | bytes 24592 | tf_op jit(solution)/shard_map/reduce_scatter | solution.py:313
  (383 shorter events, 183.2 us)
Async XLA Ops:
  7.2 1.6 copy-start
  7.2 166.6 %copy-start.23 = (f32[4]{0:T(128)S(1)}, f32[4]{0:T(128)}, u32[]{:S(2)}) copy-start(f32[4]{0:T(128)} %param.22) | copy-start | bytes 52
  7.2 168.6 %copy-start.20 = (f32[256]{0:T(256)S(1)}, f32[256]{0:T(256)}, u32[]{:S(2)}) copy-start(f32[256]{0:T(256)} %param.23) | copy-start | bytes 3076
  7.2 168.6 %copy-start.10 = (bf16[256,512]{1,0:T(8,128)(2,1)S(1)}, bf16[256,512]{1,0:T(8,128)(2,1)}, u32[]{:S(2)}) copy-start(bf16[256,512]{1,0:T(8,128)(2,1)} %param.25) | copy-start | bytes 786436
  7.2 168.6 %copy-start.9 = (bf16[512,256]{1,0:T(8,128)(2,1)S(1)}, bf16[512,256]{1,0:T(8,128)(2,1)}, u32[]{:S(2)}) copy-start(bf16[512,256]{1,0:T(8,128)(2,1)} %param.24) | copy-start | bytes 786436
  7.2 100.0 %all-gather.6.cloned.1.call-start = ((), (), s32[]{:S(2)}) async-start(), calls=%async_computation.7 | async-start | bytes 8519680 | tf_op jit(solution)/shard_map/all_gather | solution.py:25
  9.6 10.0 %collective-permute-start = (f32[3,2,256]{2,0,1:T(4,128)S(1)}, f32[3,2,256]{2,0,1:T(4,128)S(1)}, u32[]{:S(2)}, u32[]{:S(2)}) collective-permute-start(f32[3,2,256]{2,0,1:T(4,128)S(1)} %convert_element_type.90), channel_id=1, source_target_pairs={{0,4},{4,8},{8,12},{12,16},{16,20},{20,24},{24,28},{28,32},{32,36}... | collective-permute-start | bytes 18440 | tf_op jit(solution)/shard_map/ppermute | solution.py:20
  16.1 159.7 %copy-start.25 = (f32[4,256]{1,0:T(4,128)}, f32[4,256]{1,0:T(4,128)S(1)}, u32[]{:S(2)}) copy-start(f32[4,256]{1,0:T(4,128)S(1)} %get-tuple-element.406) | copy-start | bytes 12292
  17.7 89.5 %copy-start.17 = (f32[1,4,2,128]{3,1,2,0:T(4,128)}, f32[1,4,2,128]{3,1,2,0:T(4,128)S(1)}, u32[]{:S(2)}) copy-start(f32[1,4,2,128]{3,1,2,0:T(4,128)S(1)} %copy.96) | copy-start | bytes 12292
  17.9 157.8 %copy-start.18 = (f32[4]{0:T(128)}, f32[4]{0:T(128)S(1)}, u32[]{:S(2)}) copy-start(f32[4]{0:T(128)S(1)} %slice_reduce_fusion) | copy-start | bytes 52
  19.3 1.3 copy-start.14
  19.3 1.3 copy-start.15
  19.3 1.3 copy-start.16
  21.0 163.7 %copy-start.2 = (bf16[256,1,1,128]{3,2,0,1:T(2,128)(2,1)}, bf16[256,1,1,128]{3,2,0,1:T(2,128)(2,1)S(1)}, u32[]{:S(2)}) copy-start(bf16[256,1,1,128]{3,2,0,1:T(2,128)(2,1)S(1)} %get-tuple-element.396) | copy-start | bytes 196612
  21.0 163.7 %copy-start.4 = (bf16[256,1,1,128]{3,2,0,1:T(2,128)(2,1)}, bf16[256,1,1,128]{3,2,0,1:T(2,128)(2,1)S(1)}, u32[]{:S(2)}) copy-start(bf16[256,1,1,128]{3,2,0,1:T(2,128)(2,1)S(1)} %get-tuple-element.395) | copy-start | bytes 196612
  22.2 243.6 %all-gather.8.cloned.1.call-start = ((), (), s32[]{:S(2)}) async-start(), calls=%async_computation.8 | async-start | bytes 8519680 | tf_op jit(solution)/shard_map/all_gather | solution.py:25
  63.7 112.1 %copy-start.11 = (pred[256,256]{1,0:T(8,128)(4,1)}, pred[256,256]{1,0:T(8,128)(4,1)S(1)}, u32[]{:S(2)}) copy-start(pred[256,256]{1,0:T(8,128)(4,1)S(1)} %iota_compare_fusion) | copy-start | bytes 196612
  63.9 111.9 %copy-start.8 = (f32[256,256]{1,0:T(8,128)}, f32[256,256]{1,0:T(8,128)S(1)}, u32[]{:S(2)}) copy-start(f32[256,256]{1,0:T(8,128)S(1)} %fusion.90) | copy-start | bytes 786436
  173.8 2.0 copy-start.12
  175.8 13.2 %copy-start.6 = (f32[256,4,64]{0,2,1:T(8,128)}, f32[256,4,64]{0,2,1:T(8,128)S(1)}, u32[]{:S(2)}) copy-start(f32[256,4,64]{0,2,1:T(8,128)S(1)} %get-tuple-element.412) | copy-start | bytes 786436
  185.9 208.9 %reduce-scatter.8.cloned.1.call-start = ((), (), s32[]{:S(2)}) async-start(), calls=%async_computation.4 | async-start | bytes 655360 | tf_op jit(solution)/shard_map/reduce_scatter | solution.py:161
  189.0 331.6 %reduce-scatter.14.cloned.1.call-start = ((), (), s32[]{:S(2)}) async-start(), calls=%async_computation.9 | async-start | bytes 532480
  189.2 186.5 %copy-start.3 = (bf16[256,1,1,128]{3,2,0,1:T(2,128)(2,1)S(1)}, bf16[256,1,1,128]{3,2,0,1:T(2,128)(2,1)}, u32[]{:S(2)}) copy-start(bf16[256,1,1,128]{3,2,0,1:T(2,128)(2,1)} %copy-done.2) | copy-start | bytes 196612
  189.2 200.4 %copy-start.1 = (bf16[512,3,256]{2,0,1:T(8,128)(2,1)S(1)}, bf16[512,3,256]{2,0,1:T(8,128)(2,1)}, u32[]{:S(2)}) copy-start(bf16[512,3,256]{2,0,1:T(8,128)(2,1)} %param.16) | copy-start | bytes 2359300
  191.2 198.4 %copy-start.5 = (bf16[256,1,256]{2,0,1:T(8,128)(2,1)S(1)}, bf16[256,1,256]{2,0,1:T(8,128)(2,1)}, u32[]{:S(2)}) copy-start(bf16[256,1,256]{2,0,1:T(8,128)(2,1)} %copy.57) | copy-start | bytes 393220
  191.2 198.8 %copy-start.19 = (bf16[512,4]{0,1:T(4,128)(2,1)S(1)}, bf16[512,4]{0,1:T(4,128)(2,1)}, u32[]{:S(2)}) copy-start(bf16[512,4]{0,1:T(4,128)(2,1)} %param.17) | copy-start | bytes 12292
  192.3 183.8 %copy-start.7 = (f32[256,4,64]{0,2,1:T(8,128)S(1)}, f32[256,4,64]{0,2,1:T(8,128)}, u32[]{:S(2)}) copy-start(f32[256,4,64]{0,2,1:T(8,128)} %copy-done.6) | copy-start | bytes 786436
  192.3 197.8 %copy-start.22 = (f32[4]{0:T(128)S(1)}, f32[4]{0:T(128)}, u32[]{:S(2)}) copy-start(f32[4]{0:T(128)} %copy-done.21) | copy-start | bytes 52
  197.8 322.7 %reduce-scatter.10.cloned.1.call-start = ((), (), s32[]{:S(2)}) async-start(), calls=%async_computation.5 | async-start | bytes 655360 | tf_op jit(solution)/shard_map/reduce_scatter | solution.py:161
  376.1 17.4 %copy-start.24 = (u32[256]{0:T(256)S(1)}, u32[256]{0:T(256)}, u32[]{:S(2)}) copy-start(u32[256]{0:T(256)} %constant.150) | copy-start | bytes 3076
  383.3 5.4 collective-permute-start.1
  391.2 207.4 %reduce-scatter.12.cloned.1.call-start = ((), (), s32[]{:S(2)}) async-start(), calls=%async_computation.6 | async-start | bytes 1597440 | tf_op jit(solution)/shard_map/reduce_scatter | solution.py:313
  (2 other events, 2.2 us)
Sparse Core Ops, SparseCore 0:
  22.3 84.9 all-gather.5
  186.0 79.6 all-gather.7
  268.2 18.1 reduce-scatter.7
  290.8 137.1 reduce-scatter.13
  431.0 25.5 reduce-scatter.9
  461.0 137.5 reduce-scatter.11
where the time goes:
time: 615 us; the launch traced here: 605 us
  waiting for transfers between devices  190 us (31%)
  blocking collectives  173 us (28%)
  other arithmetic  139 us (23%)
  local copies, waits for them, and re-layouts  55.6 us (9%)
  matrix products  20.9 us (3%)
  between operations  15.4 us (3%)
  starting transfers between devices  7.33 us (1%)
    select_n x128, other arithmetic, hop(): return jax.tree.map(lambda a, b: jnp.where(reached, a, b), new, before)  127 us
    unnamed x1, blocking collectives  123 us
    all_gather x2, waiting for transfers between devices, carried_in(): everything = jax.tree.map(lambda part: lax.all_gather(part, axis), x)  110 us
    reduce_scatter x1, waiting for transfers between devices, body(): lax.psum_scatter(grad_in, 'tm', scatter_dimension=0, tiled=True)  78.1 us
    exp x128, local copies, waits for them, and re-layouts, link_states(): jnp.exp(later_part[0])[:, None, None] * earlier_part[1] + later_part[1]  44.7 us
    all_gather x1, blocking collectives, carried_in(): everything = jax.tree.map(lambda part: lax.all_gather(part, axis), x)  41.4 us
  transfers between devices with their start and end apart: 8, of which 4 were waited for; matrix products, arithmetic and copies ran while one was open for 24% of the time, Pallas kernels for 0%

commit v1 on v0

v1 whole, which is shorter than its diff:
```python
import functools

import jax
import jax.numpy as jnp
from jax import lax
from jax.experimental import pallas as pl
from jax.experimental.pallas import tpu as pltpu
from jax.sharding import PartitionSpec as P

N = 128
KW = 4
E = 1024
EPS = 1e-05
MESH = pl.DeviceIdType.MESH
F32 = jnp.float32
BF16 = jnp.bfloat16

RIM, DEC, SCAN1, BACK1, NORM, LAYER, SCAN2, BACK2, RIM2, WSUM1, WSUM2, ROWS = range(12)


def bf(v):
    return v.astype(BF16)


def mm(a, b, ca=1, cb=0):
    return lax.dot_general(
        bf(a), bf(b), (((ca,), (cb,)), ((), ())), preferred_element_type=F32
    )


def parts_of(v, count):
    parts = []
    for _ in range(count):
        head = bf(v)
        parts.append(head)
        v = v - head.astype(F32)
    return parts


def mm_left(exact, v, ca=1, cb=0, count=3):
    total = None
    for part in parts_of(v, count):
        term = mm(exact, part, ca, cb)
        total = term if total is None else total + term
    return total


def mm_right(v, exact, ca=1, cb=0, count=3):
    total = None
    for part in parts_of(v, count):
        term = mm(part, exact, ca, cb)
        total = term if total is None else total + term
    return total


def sigmoid(v):
    return 1.0 / (1.0 + jnp.exp(-v))


def softplus(v):
    return jnp.maximum(v, 0.0) + jnp.log1p(jnp.exp(-jnp.abs(v)))


def spread(scalars, shape, width):
    lane = lax.broadcasted_iota(jnp.int32, shape, 1) // width
    out = jnp.zeros(shape, F32)
    for h in range(scalars.shape[0]):
        out = jnp.where(lane == h, scalars[h], out)
    return out


def kernel(
    n_tm,
    n_head,
    series,
    w_in,
    w_dt,
    step_bias,
    log_rate,
    conv_w,
    conv_b,
    skip_gain,
    norm_gain,
    w_out,
    cot,
    layer_ref,
    rows_ref,
    w_in_ref,
    w_dt_ref,
    w_out_ref,
    rim_in,
    dec_send,
    dec_all,
    state_send,
    state_all,
    prefix_send,
    prefix_all,
    back_send,
    back_all,
    suffix_send,
    suffix_all,
    flat_state,
    own_keep,
    incoming,
    norm_send,
    norm_all,
    layer_send,
    layer_all,
    grow_send,
    grow_all,
    rim2_send,
    rim2_in,
    sum1_send,
    sum1_all,
    sum2_send,
    sum2_all,
    pre_buf,
    conv_buf,
    decays,
    inside_buf,
    gproj,
    send_sem,
    recv_sem,
):
    me = lax.axis_index("tm")
    mine = lax.axis_index("head")
    rows, inner = series.shape[0], w_out.shape[1]
    heads = step_bias.shape[0]
    size = inner // heads
    model = series.shape[1]
    per_owner = inner // n_tm
    owners_per_head = n_tm // heads
    quarter = rows // n_head

    barrier = pltpu.get_barrier_semaphore()

    def greet(d, c):
        pl.semaphore_signal(
            barrier, inc=1, device_id=(lax.rem(me + d, n_tm), mine), device_id_type=MESH
        )
        return c

    lax.fori_loop(1, n_tm, greet, 0)
    for d in range(1, n_head):
        pl.semaphore_signal(
            barrier, inc=1, device_id=(me, lax.rem(mine + d, n_head)), device_id_type=MESH
        )

    def push(src, dst, which, device):
        pltpu.make_async_remote_copy(
            src_ref=src,
            dst_ref=dst,
            send_sem=send_sem.at[which],
            recv_sem=recv_sem.at[which],
            device_id=device,
            device_id_type=MESH,
        ).start()

    def arrived(ref, which):
        pltpu.make_async_copy(ref, ref, recv_sem.at[which]).wait()

    def departed(ref, which):
        pltpu.make_async_copy(ref, ref, send_sem.at[which]).wait()

    def to_all(source_of, dst, which):
        def one(d, c):
            peer = lax.rem(me + d, n_tm)
            push(source_of(peer), dst.at[me], which, (peer, mine))
            return c

        lax.fori_loop(1, n_tm, one, 0)

    def to_heads(source_of, dst, which):
        for d in range(1, n_head):
            peer = lax.rem(mine + d, n_head)
            push(source_of(peer), dst.at[mine], which, (me, peer))

    expand = (
        lax.broadcasted_iota(jnp.int32, (heads, inner), 1) // size
        == lax.broadcasted_iota(jnp.int32, (heads, inner), 0)
    ).astype(BF16)
    narrow_eye = (
        lax.broadcasted_iota(jnp.int32, (heads, N), 1)
        == lax.broadcasted_iota(jnp.int32, (heads, N), 0)
    ).astype(BF16)
    w_dt_wide = bf(mm(w_dt[...], expand))
    w_dt_narrow = bf(mm(w_dt[...], narrow_eye))
    rate_wide = jnp.exp(spread(log_rate, (1, inner), size))
    skip_wide = spread(skip_gain, (1, inner), size)
    step = softplus(mm(series[...], w_dt_wide) + spread(step_bias, (1, inner), size))
    row_id = lax.broadcasted_iota(jnp.int32, (rows, rows), 0)
    col_id = lax.broadcasted_iota(jnp.int32, (rows, rows), 1)
    below = col_id <= row_id
    run = mm_left(below.astype(BF16), -step * rate_wide)
    last = run[rows - 1 : rows, :]
    for h in range(heads):
        dec_send[h] = jnp.broadcast_to(last[:, h * size : h * size + 1], (1, N))

    pl.semaphore_wait(barrier, n_tm - 1 + n_head - 1)
    nxt, prv = lax.rem(me + 1, n_tm), lax.rem(me + n_tm - 1, n_tm)
    push(series.at[pl.ds(rows - 16, 16)], rim_in, RIM, (nxt, mine))
    to_all(lambda peer: dec_send.at[peer // owners_per_head], dec_all, DEC)
    dec_all[me] = dec_send[me // owners_per_head]

    projected = bf(mm(series[...], w_in[...])).astype(F32)
    gate = projected[:, :inner]
    pre_buf[pl.ds(8, rows), :] = projected[:, inner:]
    gate_sig = sigmoid(gate)
    gate_act = gate * gate_sig
    gain_grad = norm_gain[...] * mm(cot[...], w_out[...])
    run_t = run.T
    step_t = step.T
    for h in range(heads):
        gap = run[:, h * size : h * size + 1] - run_t[h * size : h * size + 1, :]
        decays[h] = jnp.exp(jnp.where(below, gap, -1e30))
    grow = jnp.exp(run)
    remain = jnp.exp(last - run)

    arrived(rim_in, RIM)
    rim = bf(mm(rim_in[...], w_in[:, inner:])).astype(F32)[8:16]
    pre_buf[pl.ds(0, 8), :] = jnp.where(me > 0, rim, 0.0)

    def conv_row(k):
        return jnp.concatenate([conv_w[k, 0:1, :], conv_w[k, 1:2, :]], axis=1)

    conv = jnp.concatenate([conv_b[0:1, :], conv_b[1:2, :]], axis=1)
    for k in range(KW):
        conv = conv + conv_row(k) * pre_buf[pl.ds(8 - (KW - 1) + k, rows), :]
    conv_sig = sigmoid(conv)
    active = bf(conv * conv_sig)
    conv_buf[...] = conv_sig * (1.0 + conv * (1.0 - conv_sig))
    x = active[:, :inner]
    b = active[:, inner : inner + N]
    c = active[:, inner + N :]
    xw = x.astype(F32)

    def exchange(own, send, everything, out_send, out_all, which, back, reverse, during):
        flat_state[...] = own

        def pack(j, k):
            send[j] = flat_state[pl.ds(per_owner * j, per_owner), :]
            return k

        lax.fori_loop(0, n_tm, pack, 0, unroll=8)
        to_all(lambda peer: send.at[peer], everything, which)
        everything[me] = send[me]
        kept = during()
        arrived(everything.at[pl.ds(0, n_tm - 1)], which)

        def hop(k, before):
            at = n_tm - 1 - k if reverse else k
            out_send[at] = before

            @pl.when(at != me)
            def _():
                push(out_send.at[at], out_all.at[me], back, (at, mine))

            return before * jnp.exp(dec_all[at]) + everything[at]

        lax.fori_loop(0, n_tm, hop, jnp.zeros((per_owner, N), F32))
        out_all[me] = out_send[me]
        return kept

    def collect(out_all, back):
        arrived(out_all.at[pl.ds(0, n_tm - 1)], back)

        def unpack(j, k):
            flat_state[pl.ds(per_owner * j, per_owner), :] = out_all[j]
            return k

        lax.fori_loop(0, n_tm, unpack, 0, unroll=8)
        return flat_state[...]

    own = mm(remain * step * xw, b, 0, 0)
    own_keep[...] = own

    def intra_forward():
        scores = mm(c, b, 1, 1)
        for h in range(heads):
            at = slice(h * size, (h + 1) * size)
            mixing = scores * decays[h] * step_t[h * size : h * size + 1, :]
            inside_buf[:, at] = mm(mixing, x[:, at])
        return scores

    def first_wait():
        arrived(dec_all.at[pl.ds(0, n_tm - 1)], DEC)
        return intra_forward()

    scores = exchange(
        own, state_send, state_all, prefix_send, prefix_all, SCAN1, BACK1, False, first_wait
    )
    start = collect(prefix_all, BACK1)
    incoming[...] = start

    ssm = inside_buf[...] + grow * mm(c, start, 1, 1)
    y = ssm + skip_wide * xw
    gated = y * gate_act
    ones = jnp.ones((8, inner), BF16)
    power = mm_left(ones, gated * gated, 1, 1, 2)
    cross = mm_left(ones, gated * gain_grad, 1, 1, 2)
    first_row = lax.broadcasted_iota(jnp.int32, (8, rows), 0) == 0
    norm_send[...] = jnp.where(first_row, power, cross)
    to_heads(lambda peer: norm_send, norm_all, NORM)
    norm_all[mine] = norm_send[...]
    arrived(norm_all.at[pl.ds(0, n_head - 1)], NORM)
    totals = norm_all[0]
    for p in range(1, n_head):
        totals = totals + norm_all[p]
    inv_row = lax.rsqrt(totals[0:1] / E + EPS)
    coef_row = inv_row * inv_row * inv_row * totals[1:2] / E
    inv = jnp.broadcast_to(inv_row, (inner, rows)).T
    coef = jnp.broadcast_to(coef_row, (inner, rows)).T
    grad_gated = inv * gain_grad - gated * coef
    grad_y = grad_gated * gate_act
    gy = bf(grad_y)
    grown = bf(grow * grad_y)
    normed = bf(gated * inv * norm_gain[...])
    grad_gate = bf(grad_gated * y * (gate_sig * (1.0 + gate * (1.0 - gate_sig))))
    gproj[:, :inner] = grad_gate

    def intra_backward():
        group = jnp.zeros((rows, rows), F32)
        for h in range(heads):
            at = slice(h * size, (h + 1) * size)
            inside_buf[:, at] = mm(scores * decays[h], gy[:, at], 0, 0)
            group = group + decays[h] * mm(gy[:, at], x[:, at], 1, 1) * (
                step_t[h * size : h * size + 1, :]
            )
        grad_c = mm(group, b) + mm(grown, start)
        grad_b = mm(group, c, 0, 0)
        part = bf(mm(normed, w_out[...], 1, 1))
        for p in range(n_head):
            layer_send[p] = part[p * quarter : (p + 1) * quarter]
        to_heads(lambda peer: layer_send.at[peer], layer_all, LAYER)
        layer_all[mine] = layer_send[mine]
        chunk = (n_tm, model // n_tm, inner)
        sum1_send[...] = bf(
            jnp.concatenate(
                [
                    mm(cot[...], normed, 0, 0).reshape(chunk),
                    mm(series[...], grad_gate, 0, 0).reshape(chunk),
                ],
                axis=1,
            )
        )
        return grad_b, grad_c

    grad_b, grad_c = exchange(
        mm(grown, c, 0, 0),
        back_send,
        back_all,
        suffix_send,
        suffix_all,
        SCAN2,
        BACK2,
        True,
        intra_backward,
    )
    to_all(lambda peer: sum1_send.at[peer], sum1_all, WSUM1)
    sum1_all[me] = sum1_send[me]
    after = collect(suffix_all, BACK2)

    back_b = inside_buf[...] + remain * mm(b, after, 1, 1)
    grad_x = skip_wide * grad_y + step * back_b
    grad_b = grad_b + mm(step * remain * xw, after)
    gc = jnp.concatenate([grad_x, grad_b, grad_c], axis=1) * conv_buf[...]
    pre_buf[pl.ds(0, rows), :] = gc
    rim2_send[...] = gc[0:8]
    push(rim2_send, rim2_in, RIM2, (prv, mine))

    choose = (
        lax.broadcasted_iota(jnp.int32, (inner, N), 0) // size
        == lax.broadcasted_iota(jnp.int32, (inner, N), 1)
    )
    pick = choose.astype(BF16)
    shift_n = mm(series[...], w_dt_narrow) + spread(step_bias, (1, N), 1)
    x_back = mm_right(xw * back_b, pick)
    grad_cum = mm_right(grad_y * ssm, pick) - softplus(shift_n) * x_back
    final = jnp.exp(run_t[:, rows - 1 : rows]) * start + own_keep[...]
    carried = jnp.sum(
        jnp.where(choose, jnp.sum(after * final, axis=1, keepdims=True), 0.0),
        axis=0,
        keepdims=True,
    )
    grad_log = mm_left((col_id >= row_id).astype(BF16), grad_cum) + carried
    rate_n = jnp.exp(spread(log_rate, (1, N), 1))
    grad_raw = bf((x_back - rate_n * grad_log) * sigmoid(shift_n))

    arrived(rim2_in, RIM2)
    pre_buf[pl.ds(rows, 8), :] = jnp.where(me < n_tm - 1, rim2_in[...], 0.0)
    grad_pre = conv_row(0) * pre_buf[pl.ds(KW - 1, rows), :]
    for k in range(1, KW):
        grad_pre = grad_pre + conv_row(k) * pre_buf[pl.ds(KW - 1 - k, rows), :]
    grad_pre = bf(grad_pre)
    gproj[:, inner:] = grad_pre

    deep = mm(series[...], grad_pre, 0, 0)
    thin = mm(series[...], grad_raw, 0, 0)
    chunk = (n_tm, model // n_tm, inner)
    sum2_send[:, :, :inner] = bf(
        jnp.concatenate(
            [deep[:, :inner].reshape(chunk), deep[:, inner:].reshape(chunk)], axis=1
        )
    )
    thin = thin.reshape(n_tm, model // n_tm, N)
    sum2_send[:, :, inner:] = bf(jnp.concatenate([thin, jnp.zeros_like(thin)], axis=1))
    to_all(lambda peer: sum2_send.at[peer], sum2_all, WSUM2)
    sum2_all[me] = sum2_send[me]

    grad_rows = bf(mm(gproj[...], w_in[...], 1, 1) + mm(grad_raw, w_dt_narrow, 1, 1))
    for p in range(n_head):
        grow_send[p] = grad_rows[p * quarter : (p + 1) * quarter]
    to_heads(lambda peer: grow_send.at[peer], grow_all, ROWS)
    grow_all[mine] = grow_send[mine]

    def over_heads(everything):
        total = everything[0].astype(F32)
        for p in range(1, n_head):
            total = total + everything[p].astype(F32)
        return total

    arrived(layer_all.at[pl.ds(0, n_head - 1)], LAYER)
    layer_ref[...] = bf(over_heads(layer_all))
    arrived(sum1_all.at[pl.ds(0, n_tm - 1)], WSUM1)
    arrived(grow_all.at[pl.ds(0, n_head - 1)], ROWS)
    rows_ref[...] = over_heads(grow_all)

    def over_slabs(everything):
        def add(k, total):
            return total + everything[k].astype(F32)

        return lax.fori_loop(0, n_tm, add, jnp.zeros(everything.shape[1:], F32), unroll=4)

    few = model // n_tm
    total1 = over_slabs(sum1_all)
    w_out_ref[...] = total1[:few]
    w_in_ref[:, :inner] = total1[few:]
    arrived(sum2_all.at[pl.ds(0, n_tm - 1)], WSUM2)
    total2 = over_slabs(sum2_all)
    w_in_ref[:, inner : 2 * inner] = total2[:few, :inner]
    w_in_ref[:, 2 * inner :] = total2[few:, :inner]
    w_dt_ref[...] = total2[:few, inner:]

    departed(rim_in, RIM)
    departed(dec_all.at[pl.ds(0, n_tm - 1)], DEC)
    departed(state_all.at[pl.ds(0, n_tm - 1)], SCAN1)
    departed(prefix_all.at[pl.ds(0, n_tm - 1)], BACK1)
    departed(norm_all.at[pl.ds(0, n_head - 1)], NORM)
    departed(layer_all.at[pl.ds(0, n_head - 1)], LAYER)
    departed(back_all.at[pl.ds(0, n_tm - 1)], SCAN2)
    departed(suffix_all.at[pl.ds(0, n_tm - 1)], BACK2)
    departed(rim2_in, RIM2)
    departed(sum1_all.at[pl.ds(0, n_tm - 1)], WSUM1)
    departed(sum2_all.at[pl.ds(0, n_tm - 1)], WSUM2)
    departed(grow_all.at[pl.ds(0, n_head - 1)], ROWS)


def solution(mesh):
    n_tm, n_head = mesh.shape["tm"], mesh.shape["head"]

    def body(
        series,
        in_weight,
        step_weight,
        step_bias,
        log_rate,
        conv_weight,
        conv_bias,
        skip_gain,
        norm_gain,
        out_weight,
        cotangent,
    ):
        rows, model = series.shape
        inner = out_weight.shape[1]
        heads = step_bias.shape[0]
        few = model // n_tm
        quarter = rows // n_head
        vmem = pl.BlockSpec(memory_space=pltpu.VMEM)
        smem = pl.BlockSpec(memory_space=pltpu.SMEM)
        slab = pltpu.VMEM((n_tm, inner // n_tm, N), F32)
        peers = pltpu.VMEM((n_head, quarter, model), BF16)
        layer, rows_grad, w_in, w_dt, w_out = pl.pallas_call(
            functools.partial(kernel, n_tm, n_head),
            out_shape=(
                jax.ShapeDtypeStruct((quarter, model), BF16),
                jax.ShapeDtypeStruct((quarter, model), F32),
                jax.ShapeDtypeStruct((few, 3 * inner), F32),
                jax.ShapeDtypeStruct((few, N), F32),
                jax.ShapeDtypeStruct((few, inner), F32),
            ),
            in_specs=[vmem, vmem, vmem, smem, smem, vmem, vmem, smem, vmem, vmem, vmem],
            out_specs=(vmem,) * 5,
            scratch_shapes=[
                pltpu.VMEM((16, model), BF16),
                pltpu.VMEM((heads, 1, N), F32),
                pltpu.VMEM((n_tm, 1, N), F32),
                slab,
                slab,
                slab,
                slab,
                slab,
                slab,
                slab,
                slab,
                pltpu.VMEM((inner, N), F32),
                pltpu.VMEM((inner, N), F32),
                pltpu.VMEM((inner, N), F32),
                pltpu.VMEM((8, rows), F32),
                pltpu.VMEM((n_head, 8, rows), F32),
                peers,
                peers,
                peers,
                peers,
                pltpu.VMEM((8, 2 * inner), F32),
                pltpu.VMEM((8, 2 * inner), F32),
                pltpu.VMEM((n_tm, 2 * few, inner), BF16),
                pltpu.VMEM((n_tm, 2 * few, inner), BF16),
                pltpu.VMEM((n_tm, 2 * few, inner + N), BF16),
                pltpu.VMEM((n_tm, 2 * few, inner + N), BF16),
                pltpu.VMEM((rows + 8, 2 * inner), F32),
                pltpu.VMEM((rows, 2 * inner), F32),
                pltpu.VMEM((heads, rows, rows), F32),
                pltpu.VMEM((rows, inner), F32),
                pltpu.VMEM((rows, 3 * inner), BF16),
                pltpu.SemaphoreType.DMA((12,)),
                pltpu.SemaphoreType.DMA((12,)),
            ],
            compiler_params=pltpu.CompilerParams(collective_id=0, has_side_effects=True),
        )(
            series,
            in_weight.reshape(model, 3 * inner),
            step_weight,
            step_bias,
            log_rate,
            conv_weight,
            conv_bias,
            skip_gain,
            norm_gain.reshape(1, inner),
            out_weight,
            cotangent,
        )
        return (layer, rows_grad, w_in.reshape(few, 3, inner), w_dt[:, :heads], w_out)

    in_specs = (
        P("tm", None),
        P(None, None, "head"),
        P(None, "head"),
        P("head"),
        P("head"),
        P(None, None, "head"),
        P(None, "head"),
        P("head"),
        P("head"),
        P(None, "head"),
        P("tm", None),
    )
    out_specs = (
        P(("tm", "head"), None),
        P(("tm", "head"), None),
        P("tm", None, "head"),
        P("tm", "head"),
        P("tm", "head"),
    )
    return jax.shard_map(body, mesh=mesh, in_specs=in_specs, out_specs=out_specs, check_vma=False)
```

time: 615 us -> 86.8 us (0.14); the launches traced: 605 us -> 86.5 us
  waiting for transfers between devices: 190 us -> 0 us
  blocking collectives: 173 us -> 0 us
  other arithmetic: 139 us -> 0 us
  Pallas kernels: 0 us -> 77.5 us
  local copies, waits for them, and re-layouts: 55.6 us -> 8.27 us
  matrix products: 20.9 us -> 0 us
  between operations: 15.4 us -> 0.66 us
  starting transfers between devices: 7.33 us -> 0 us
    select_n x128 -> x0, other arithmetic: 127 us -> none  [hop(): return jax.tree.map(lambda a, b: jnp.where(reached, a, b), new, before)]
    unnamed x1 -> x0, blocking collectives: 123 us -> none
    all_gather x2 -> x0, waiting for transfers between devices: 110 us -> none  [carried_in(): everything = jax.tree.map(lambda part: lax.all_gather(part, axis), x)]
    reduce_scatter x3 -> x0, waiting for transfers between devices: 78.1 us -> none  [the longest x1 78.1 us: body(): lax.psum_scatter(grad_in, 'tm', scatter_dimension=0, tiled=True)]
    pallas_call x0 -> x1, Pallas kernels: none -> 77.5 us  [body(): pl.pallas_call(functools.partial(kernel, n_tm, n_head), out_shape=(jax.Sh...]
    exp x130 -> x0, local copies, waits for them, and re-layouts: 46.5 us -> none  [the longest x128 44.7 us: link_states(): jnp.exp(later_part[0])[:, None, None] * earlier_part[1] + later_part[1]]
    all_gather x1 -> x0, blocking collectives: 41.4 us -> none  [carried_in(): everything = jax.tree.map(lambda part: lax.all_gather(part, axis), x)]
    dot_general x22 -> x0, matrix products: 20.9 us -> none  [the longest x6 5.19 us: contract(): lax.dot_general(left_side, right_side, (((left_dim,), (right_dim,)), ((),...]
  transfers between devices with their start and end apart: 8 -> 0, of which waited for: 4 -> 0; matrix products, arithmetic and copies ran while one was open for 24% -> 0% of each run, Pallas kernels for 0% -> 0%
where the time goes in v1:
time: 86.8 us; the launch traced here: 86.5 us
  Pallas kernels  77.5 us (89%)
  local copies, waits for them, and re-layouts  8.27 us (10%)
    pallas_call x1, Pallas kernels, body(): pl.pallas_call(functools.partial(kernel, n_tm, n_head), out_shape=(jax.Sh...  77.5 us
    unnamed x15, local copies, waits for them, and re-layouts  7.11 us

profile of v1, /device:TPU:1, one launch (start us, length us, event | category | flops | bytes accessed | tf_op | source)
XLA Modules:
  0.0 86.5 jit_solution(15659957435993760566)
XLA Ops:
  0.6 1.4 %copy.19 = bf16[512,3,256]{0,2,1:T(8,128)(2,1)S(1)} copy(bf16[512,3,256]{2,0,1:T(8,128)(2,1)} %param.12) | data formatting | bytes 1572864 | tf_op args[1]
  2.0 0.0 copy-start.3
  2.1 1.2 %copy.20.w_in = bf16[512,768]{1,0:T(8,128)(2,1)} copy(bf16[512,768]{0,1:T(8,128)(2,1)S(1)} %bitcast.4) | data formatting | bytes 1572864 | tf_op jit(solution)/shard_map/reshape | solution.py:532
  3.2 0.0 copy-done.3
  3.2 0.8 copy.21.w_dt
  4.0 77.5 %shard_map.146 = (bf16[64,512]{1,0:T(8,128)(2,1)}, f32[64,512]{1,0:T(8,128)}, f32[8,768]{1,0:T(8,128)}, f32[8,128]{1,0:T(8,128)}, f32[8,256]{1,0:T(8,128)}) custom-call(bf16[256,512]{1,0:T(8,128)(2,1)} %series.1, bf16[512,768]{1,0:T(8,128)(2,1)} %copy.20.w_in, bf16[512,4]{1,0:T(8,128)(2,1)} %copy.21.w_dt, f32[4]{0:T(128)} %step_bias.1, f32[4]{0:T(128)} %log_rate.1, ...), custom_call_target="tpu_custom_call" | custom-call | tf_op jit(solution)/shard_map/pallas_call | solution.py:483
  81.6 0.0 copy-start
  81.6 1.4 %copy.22 = f32[8,4]{0,1:T(4,128)} copy(f32[8,4]{1,0:T(8,128)} %bitcast.6) | data formatting | bytes 256
  82.9 1.5 %copy.27 = bf16[64,512]{1,0:T(8,128)(2,1)} copy(bf16[64,512]{1,0:T(8,128)(2,1)} %get-tuple-element.30) | data formatting | bytes 131072
  84.4 0.0 copy-done
  84.4 0.0 copy-start.1
  84.4 0.7 copy.28
  85.1 0.1 copy-done.1
  85.2 0.0 copy-start.2
  85.2 0.6 copy.29
  85.8 0.1 copy-done.2
  85.9 0.6 copy.30
Async XLA Ops:
  2.0 1.2 %copy-start.3 = (bf16[512,4]{0,1:T(4,128)(2,1)S(1)}, bf16[512,4]{0,1:T(4,128)(2,1)}, u32[]{:S(2)}) copy-start(bf16[512,4]{0,1:T(4,128)(2,1)} %param.13) | copy-start | bytes 12292
  81.6 2.8 %copy-start = (f32[64,512]{1,0:T(8,128)S(1)}, f32[64,512]{1,0:T(8,128)}, u32[]{:S(2)}) copy-start(f32[64,512]{1,0:T(8,128)} %get-tuple-element.31) | copy-start | bytes 393220
  84.4 0.7 copy-start.1
  85.2 0.7 copy-start.2

commit v2 on v1

v2 whole, which is shorter than its diff:
```python
import functools

import jax
import jax.numpy as jnp
from jax import lax
from jax.experimental import pallas as pl
from jax.experimental.pallas import tpu as pltpu
from jax.sharding import PartitionSpec as P

N = 128
KW = 4
E = 1024
EPS = 1e-05
MESH = pl.DeviceIdType.MESH
F32 = jnp.float32
BF16 = jnp.bfloat16

NZ = 8
RIM, DEC, SCAN1, BACK1, NORM, LAYER, SCAN2, BACK2, RIM2, ROWS = range(10)
CORE1, ALONG_Y1, ALONG_Z1, CORE2, ALONG_Y2, ALONG_Z2 = range(10, 16)
LOADS = 8


def bf(v):
    return v.astype(BF16)


def mm(a, b, ca=1, cb=0):
    return lax.dot_general(
        bf(a), bf(b), (((ca,), (cb,)), ((), ())), preferred_element_type=F32
    )


def parts_of(v, count):
    parts = []
    for _ in range(count):
        head = bf(v)
        parts.append(head)
        v = v - head.astype(F32)
    return parts


def mm_left(exact, v, ca=1, cb=0, count=3):
    total = None
    for part in parts_of(v, count):
        term = mm(exact, part, ca, cb)
        total = term if total is None else total + term
    return total


def mm_right(v, exact, ca=1, cb=0, count=3):
    total = None
    for part in parts_of(v, count):
        term = mm(part, exact, ca, cb)
        total = term if total is None else total + term
    return total


def sigmoid(v):
    return 1.0 / (1.0 + jnp.exp(-v))


def softplus(v):
    return jnp.maximum(v, 0.0) + jnp.log1p(jnp.exp(-jnp.abs(v)))


def spread(scalars, shape, width):
    lane = lax.broadcasted_iota(jnp.int32, shape, 1) // width
    out = jnp.zeros(shape, F32)
    for h in range(scalars.shape[0]):
        out = jnp.where(lane == h, scalars[h], out)
    return out


def kernel(
    n_tm,
    n_head,
    step_bias,
    log_rate,
    skip_gain,
    series_hbm,
    w_in_hbm,
    w_dt_hbm,
    conv_w_hbm,
    conv_b_hbm,
    norm_gain_hbm,
    w_out_hbm,
    cot_hbm,
    layer_ref,
    rows_ref,
    w_in_ref,
    w_dt_ref,
    w_out_ref,
    series,
    w_in,
    w_dt,
    conv_w,
    conv_b,
    norm_gain,
    w_out,
    cot,
    rim_in,
    dec_send,
    dec_all,
    state_send,
    state_all,
    prefix_send,
    prefix_all,
    back_send,
    back_all,
    suffix_send,
    suffix_all,
    flat_state,
    own_keep,
    norm_send,
    norm_all,
    layer_send,
    layer_all,
    grow_send,
    grow_all,
    rim2_send,
    rim2_in,
    core1_send,
    core1_in,
    y1_send,
    y1_all,
    z1_send,
    z1_all,
    core2_send,
    core2_in,
    y2_send,
    y2_all,
    z2_send,
    z2_all,
    pre_buf,
    conv_buf,
    act_buf,
    decays,
    inside_buf,
    load_sem,
    send_sem,
    recv_sem,
):
    me = lax.axis_index("tm")
    mine = lax.axis_index("head")
    core = lax.rem(me, 2)
    chip = me // 2
    at_z = lax.rem(chip, NZ)
    at_y = chip // NZ
    n_chip = n_tm // 2
    n_y = n_chip // NZ
    rows, model = series.shape
    inner = w_out.shape[1]
    heads = step_bias.shape[0]
    size = inner // heads
    per_owner = inner // n_tm
    owners_per_head = n_tm // heads
    quarter = rows // n_head
    few = model // n_tm

    barrier = pltpu.get_barrier_semaphore()

    def around(k):
        return lax.rem(me + 1 + lax.rem(k + 3 * n_tm // 8 - 1, n_tm - 1), n_tm)

    def greet(k, c):
        pl.semaphore_signal(barrier, inc=1, device_id=(around(k), mine), device_id_type=MESH)
        return c

    lax.fori_loop(0, n_tm - 1, greet, 0)
    for d in range(1, n_head):
        pl.semaphore_signal(
            barrier, inc=1, device_id=(me, lax.rem(mine + d, n_head)), device_id_type=MESH
        )
    loads = [
        pltpu.make_async_copy(src, dst, load_sem.at[k])
        for k, (src, dst) in enumerate(
            [
                (w_dt_hbm, w_dt),
                (series_hbm, series),
                (w_in_hbm, w_in),
                (conv_w_hbm, conv_w),
                (conv_b_hbm, conv_b),
                (cot_hbm, cot),
                (w_out_hbm, w_out),
                (norm_gain_hbm, norm_gain),
            ]
        )
    ]
    for load in loads:
        load.start()

    def push(src, dst, which, device):
        pltpu.make_async_remote_copy(
            src_ref=src,
            dst_ref=dst,
            send_sem=send_sem.at[which],
            recv_sem=recv_sem.at[which],
            device_id=device,
            device_id_type=MESH,
        ).start()

    def arrived(ref, which):
        pltpu.make_async_copy(ref, ref, recv_sem.at[which]).wait()

    def departed(ref, which):
        pltpu.make_async_copy(ref, ref, send_sem.at[which]).wait()

    def to_all(source_of, dst, which):
        def one(k, c):
            peer = around(k)
            push(source_of(peer), dst.at[me], which, (peer, mine))
            return c

        lax.fori_loop(0, n_tm - 1, one, 0)

    def to_heads(source_of, dst, which):
        for d in (2, 1, 3):
            peer = lax.rem(mine + d, n_head)
            push(source_of(peer), dst.at[mine], which, (me, peer))

    def chosen(width, per):
        return (
            lax.broadcasted_iota(jnp.int32, (width, heads), 0) // per
            == lax.broadcasted_iota(jnp.int32, (width, heads), 1)
        ).astype(BF16)

    rate_wide = jnp.exp(spread(log_rate, (1, inner), size))
    skip_wide = spread(skip_gain, (1, inner), size)
    row_id = lax.broadcasted_iota(jnp.int32, (rows, rows), 0)
    col_id = lax.broadcasted_iota(jnp.int32, (rows, rows), 1)
    below = col_id <= row_id
    loads[0].wait()
    w_dt_wide = bf(mm(chosen(inner, size), w_dt[...]))
    w_dt_rows = bf(mm(chosen(N, 1), w_dt[...]))
    loads[1].wait()
    step = softplus(mm(series[...], w_dt_wide, 1, 1) + spread(step_bias, (1, inner), size))
    shift_n = mm(series[...], w_dt_rows, 1, 1) + spread(step_bias, (1, N), 1)
    run = mm_left(below.astype(BF16), -step * rate_wide)
    last = run[rows - 1 : rows, :]
    for h in range(heads):
        dec_send[h] = jnp.broadcast_to(last[:, h * size : h * size + 1], (1, N))
    loads[2].wait()
    gate = bf(mm(series[...], w_in[0])).astype(F32)
    pre_buf[pl.ds(0, 8), :] = jnp.zeros((8, 2 * inner), F32)
    pre_buf[pl.ds(8, rows), :inner] = bf(mm(series[...], w_in[1])).astype(F32)
    pre_buf[pl.ds(8, rows), inner:] = bf(mm(series[...], w_in[2])).astype(F32)
    gate_sig = sigmoid(gate)
    gate_act = gate * gate_sig
    run_t = run.T
    step_t = step.T
    remain = jnp.exp(last - run)
    grow = jnp.exp(run)
    weight = remain * step

    def conv_row(k):
        return jnp.concatenate([conv_w[k, 0:1, :], conv_w[k, 1:2, :]], axis=1)

    loads[3].wait()
    loads[4].wait()

    def convolve(count):
        conv = jnp.concatenate([conv_b[0:1, :], conv_b[1:2, :]], axis=1)
        for k in range(KW):
            conv = conv + conv_row(k) * pre_buf[pl.ds(8 - (KW - 1) + k, count), :]
        conv_sig = sigmoid(conv)
        conv_buf[pl.ds(0, count), :] = conv_sig * (1.0 + conv * (1.0 - conv_sig))
        active = bf(conv * conv_sig).astype(F32)
        act_buf[pl.ds(0, count), :] = active
        return active

    active = convolve(rows)
    first = 16
    later = lax.broadcasted_iota(jnp.int32, (rows, inner), 0) >= first
    own = mm(jnp.where(later, weight * active[:, :inner], 0.0), active[:, inner : inner + N], 0, 0)
    loads[5].wait()
    loads[6].wait()
    loads[7].wait()
    gain_grad = norm_gain[...] * mm(cot[...], w_out[...])
    for h in range(heads):
        gap = run[:, h * size : h * size + 1] - run_t[h * size : h * size + 1, :]
        decays[h] = jnp.exp(jnp.where(below, gap, -1e30))

    pl.semaphore_wait(barrier, n_tm - 1 + n_head - 1)
    nxt, prv = lax.rem(me + 1, n_tm), lax.rem(me + n_tm - 1, n_tm)
    push(series.at[pl.ds(rows - 16, 16)], rim_in, RIM, (nxt, mine))
    to_all(lambda peer: dec_send.at[peer // owners_per_head], dec_all, DEC)
    dec_all[me] = dec_send[me // owners_per_head]

    arrived(rim_in, RIM)
    for s in (1, 2):
        rim = bf(mm(rim_in[...], w_in[s])).astype(F32)[8:16]
        pre_buf[pl.ds(0, 8), pl.ds((s - 1) * inner, inner)] = jnp.where(me > 0, rim, 0.0)
    active = convolve(first)
    own = own + mm(weight[:first] * active[:, :inner], active[:, inner : inner + N], 0, 0)

    def exchange(own, send, everything, out_send, out_all, which, back, reverse, during):
        flat_state[...] = own

        def pack(j, k):
            send[j] = flat_state[pl.ds(per_owner * j, per_owner), :]
            return k

        lax.fori_loop(0, n_tm, pack, 0, unroll=8)
        to_all(lambda peer: send.at[peer], everything, which)
        everything[me] = send[me]
        kept = during()
        arrived(everything.at[pl.ds(0, n_tm - 1)], which)

        def hop(k, before):
            at = n_tm - 1 - k if reverse else k
            out_send[at] = before

            @pl.when(at != me)
            def _():
                push(out_send.at[at], out_all.at[me], back, (at, mine))

            return before * jnp.exp(dec_all[at]) + everything[at]

        lax.fori_loop(0, n_tm, hop, jnp.zeros((per_owner, N), F32))
        out_all[me] = out_send[me]
        return kept

    def collect(out_all, back):
        arrived(out_all.at[pl.ds(0, n_tm - 1)], back)

        def unpack(j, k):
            flat_state[pl.ds(per_owner * j, per_owner), :] = out_all[j]
            return k

        lax.fori_loop(0, n_tm, unpack, 0, unroll=8)
        return flat_state[...]

    def by_chip(left, right, send, lanes):
        shape = (n_chip, 2, few, left.shape[1])
        left, right = left.reshape(shape), right.reshape(shape)
        for p in range(2):
            send[p, :, :, lanes] = bf(jnp.concatenate([left[:, p], right[:, p]], axis=1))

    def core_stage(send, into, which):
        push(send.at[1 - core], into, which, (me + 1 - 2 * core, mine))

    def y_stage(core_send, core_in, send, everything, which, core_which):
        arrived(core_in, core_which)
        send[...] = bf(core_send[core].astype(F32) + core_in[...].astype(F32)).reshape(send.shape)
        for d in (2, 1, 3):
            peer = lax.rem(at_y + d, n_y)
            push(
                send.at[peer],
                everything.at[at_y],
                which,
                ((peer * NZ + at_z) * 2 + core, mine),
            )

    def z_stage(y_send, y_all, send, everything, which, y_which):
        arrived(y_all.at[pl.ds(0, n_y - 1)], y_which)
        total = y_send[at_y].astype(F32)
        for d in range(1, n_y):
            total = total + y_all[lax.rem(at_y + d, n_y)].astype(F32)
        send[...] = bf(total)
        for d in (4, 3, 5, 2, 6, 1, 7):
            peer = lax.rem(at_z + d, NZ)
            push(
                send.at[peer],
                everything.at[at_z],
                which,
                ((at_y * NZ + peer) * 2 + core, mine),
            )

    def last_stage(z_send, z_all, which):
        arrived(z_all.at[pl.ds(0, NZ - 1)], which)
        total = z_send[at_z].astype(F32)
        for d in range(1, NZ):
            total = total + z_all[lax.rem(at_z + d, NZ)].astype(F32)
        return total

    own_keep[...] = own

    def intra_forward():
        x = bf(act_buf[:, :inner])
        b = bf(act_buf[:, inner : inner + N])
        c = bf(act_buf[:, inner + N :])
        scores = mm(c, b, 1, 1)
        for h in range(heads):
            at = slice(h * size, (h + 1) * size)
            mixing = scores * decays[h] * step_t[h * size : h * size + 1, :]
            inside_buf[:, at] = mm(mixing, x[:, at])
        arrived(dec_all.at[pl.ds(0, n_tm - 1)], DEC)
        return x, b, c, scores

    x, b, c, scores = exchange(
        own, state_send, state_all, prefix_send, prefix_all, SCAN1, BACK1, False, intra_forward
    )
    xw = x.astype(F32)
    start = collect(prefix_all, BACK1)

    ssm = inside_buf[...] + grow * mm(c, start, 1, 1)
    y = ssm + skip_wide * xw
    gated = y * gate_act
    ones = jnp.ones((8, inner), BF16)
    power = mm_left(ones, gated * gated, 1, 1, 2)
    cross = mm_left(ones, gated * gain_grad, 1, 1, 2)
    first_row = lax.broadcasted_iota(jnp.int32, (8, rows), 0) == 0
    norm_send[...] = jnp.where(first_row, power, cross)
    to_heads(lambda peer: norm_send, norm_all, NORM)
    norm_all[mine] = norm_send[...]
    arrived(norm_all.at[pl.ds(0, n_head - 1)], NORM)
    totals = norm_all[0]
    for p in range(1, n_head):
        totals = totals + norm_all[p]
    inv_row = lax.rsqrt(totals[0:1] / E + EPS)
    coef_row = inv_row * inv_row * inv_row * totals[1:2] / E
    inv = jnp.broadcast_to(inv_row, (inner, rows)).T
    coef = jnp.broadcast_to(coef_row, (inner, rows)).T
    grad_gated = inv * gain_grad - gated * coef
    grad_y = grad_gated * gate_act
    gy = bf(grad_y)
    grown = bf(grow * grad_y)

    def intra_backward():
        normed = bf(gated * inv * norm_gain[...])
        grad_gate = bf(grad_gated * y * (gate_sig * (1.0 + gate * (1.0 - gate_sig))))
        by_chip(
            mm(cot[...], normed, 0, 0),
            mm(series[...], grad_gate, 0, 0),
            core1_send,
            slice(None),
        )
        core_stage(core1_send, core1_in, CORE1)
        part = bf(mm(normed, w_out[...], 1, 1))
        for p in range(n_head):
            layer_send[p] = part[p * quarter : (p + 1) * quarter]
        to_heads(lambda peer: layer_send.at[peer], layer_all, LAYER)
        layer_all[mine] = layer_send[mine]
        group = jnp.zeros((rows, rows), F32)
        for h in range(heads):
            at = slice(h * size, (h + 1) * size)
            inside_buf[:, at] = mm(scores * decays[h], gy[:, at], 0, 0)
            group = group + decays[h] * mm(gy[:, at], x[:, at], 1, 1) * (
                step_t[h * size : h * size + 1, :]
            )
        grad_c = mm(group, b) + mm(grown, start)
        grad_b = mm(group, c, 0, 0)
        return grad_b, grad_c, grad_gate

    grad_b, grad_c, grad_gate = exchange(
        mm(grown, c, 0, 0),
        back_send,
        back_all,
        suffix_send,
        suffix_all,
        SCAN2,
        BACK2,
        True,
        intra_backward,
    )
    after = collect(suffix_all, BACK2)
    y_stage(core1_send, core1_in, y1_send, y1_all, ALONG_Y1, CORE1)

    back_b = inside_buf[...] + remain * mm(b, after, 1, 1)
    grad_x = skip_wide * grad_y + step * back_b
    grad_b = grad_b + mm(weight * xw, after)
    gc = jnp.concatenate([grad_x, grad_b, grad_c], axis=1) * conv_buf[...]
    pre_buf[pl.ds(0, rows), :] = gc
    rim2_send[...] = gc[0:8]
    push(rim2_send, rim2_in, RIM2, (prv, mine))

    choose = (
        lax.broadcasted_iota(jnp.int32, (inner, N), 0) // size
        == lax.broadcasted_iota(jnp.int32, (inner, N), 1)
    )
    pick = choose.astype(BF16)
    x_back = mm_right(xw * back_b, pick)
    grad_cum = mm_right(grad_y * ssm, pick) - softplus(shift_n) * x_back
    final = jnp.exp(run_t[:, rows - 1 : rows]) * start + own_keep[...]
    carried = jnp.sum(
        jnp.where(choose, jnp.sum(after * final, axis=1, keepdims=True), 0.0),
        axis=0,
        keepdims=True,
    )
    grad_log = mm_left((col_id >= row_id).astype(BF16), grad_cum) + carried
    rate_n = jnp.exp(spread(log_rate, (1, N), 1))
    grad_raw = bf((x_back - rate_n * grad_log) * sigmoid(shift_n))
    thin = mm(series[...], grad_raw, 0, 0)
    by_chip(thin, jnp.zeros_like(thin), core2_send, slice(inner, inner + N))

    arrived(rim2_in, RIM2)
    pre_buf[pl.ds(rows, 8), :] = jnp.where(me < n_tm - 1, rim2_in[...], 0.0)
    grad_pre = conv_row(0) * pre_buf[pl.ds(KW - 1, rows), :]
    for k in range(1, KW):
        grad_pre = grad_pre + conv_row(k) * pre_buf[pl.ds(KW - 1 - k, rows), :]
    grad_pre = bf(grad_pre)
    by_chip(
        mm(series[...], grad_pre[:, :inner], 0, 0),
        mm(series[...], grad_pre[:, inner:], 0, 0),
        core2_send,
        slice(0, inner),
    )
    core_stage(core2_send, core2_in, CORE2)

    grad_rows = bf(
        mm(grad_gate, w_in[0], 1, 1)
        + mm(grad_pre[:, :inner], w_in[1], 1, 1)
        + mm(grad_pre[:, inner:], w_in[2], 1, 1)
        + mm(grad_raw, w_dt_rows)
    )
    for p in range(n_head):
        grow_send[p] = grad_rows[p * quarter : (p + 1) * quarter]
    to_heads(lambda peer: grow_send.at[peer], grow_all, ROWS)
    grow_all[mine] = grow_send[mine]

    def over_heads(everything):
        total = everything[0].astype(F32)
        for p in range(1, n_head):
            total = total + everything[p].astype(F32)
        return total

    y_stage(core2_send, core2_in, y2_send, y2_all, ALONG_Y2, CORE2)
    z_stage(y1_send, y1_all, z1_send, z1_all, ALONG_Z1, ALONG_Y1)
    arrived(layer_all.at[pl.ds(0, n_head - 1)], LAYER)
    layer_ref[...] = bf(over_heads(layer_all))
    z_stage(y2_send, y2_all, z2_send, z2_all, ALONG_Z2, ALONG_Y2)
    total1 = last_stage(z1_send, z1_all, ALONG_Z1)
    w_out_ref[...] = total1[:few]
    w_in_ref[0] = total1[few:]
    arrived(grow_all.at[pl.ds(0, n_head - 1)], ROWS)
    rows_ref[...] = over_heads(grow_all)
    total2 = last_stage(z2_send, z2_all, ALONG_Z2)
    w_in_ref[1] = total2[:few, :inner]
    w_in_ref[2] = total2[few:, :inner]
    w_dt_ref[...] = total2[:few, inner:].T[:heads]

    departed(rim_in, RIM)
    departed(dec_all.at[pl.ds(0, n_tm - 1)], DEC)
    departed(state_all.at[pl.ds(0, n_tm - 1)], SCAN1)
    departed(prefix_all.at[pl.ds(0, n_tm - 1)], BACK1)
    departed(norm_all.at[pl.ds(0, n_head - 1)], NORM)
    departed(layer_all.at[pl.ds(0, n_head - 1)], LAYER)
    departed(back_all.at[pl.ds(0, n_tm - 1)], SCAN2)
    departed(suffix_all.at[pl.ds(0, n_tm - 1)], BACK2)
    departed(rim2_in, RIM2)
    departed(grow_all.at[pl.ds(0, n_head - 1)], ROWS)
    departed(core1_in, CORE1)
    departed(core2_in, CORE2)
    departed(y1_all.at[pl.ds(0, n_y - 1)], ALONG_Y1)
    departed(y2_all.at[pl.ds(0, n_y - 1)], ALONG_Y2)
    departed(z1_all.at[pl.ds(0, NZ - 1)], ALONG_Z1)
    departed(z2_all.at[pl.ds(0, NZ - 1)], ALONG_Z2)


def hand_over(*refs):
    half = len(refs) // 2
    for src, dst in zip(refs[:half], refs[half:]):
        dst[...] = src[...]


def solution(mesh):
    n_tm, n_head = mesh.shape["tm"], mesh.shape["head"]

    def body(
        series,
        in_weight,
        step_weight,
        step_bias,
        log_rate,
        conv_weight,
        conv_bias,
        skip_gain,
        norm_gain,
        out_weight,
        cotangent,
    ):
        rows, model = series.shape
        inner = out_weight.shape[1]
        heads = step_bias.shape[0]
        few = model // n_tm
        quarter = rows // n_head
        n_chip = n_tm // 2
        n_y = n_chip // NZ
        vmem = pl.BlockSpec(memory_space=pltpu.VMEM)
        smem = pl.BlockSpec(memory_space=pltpu.SMEM)
        left = pl.BlockSpec(memory_space=pl.ANY)
        arrays = (
            series,
            in_weight.transpose(1, 0, 2),
            step_weight.T,
            conv_weight,
            conv_bias,
            norm_gain.reshape(1, inner),
            out_weight,
            cotangent,
        )
        out_shape = (
            jax.ShapeDtypeStruct((quarter, model), BF16),
            jax.ShapeDtypeStruct((quarter, model), F32),
            jax.ShapeDtypeStruct((3, few, inner), F32),
            jax.ShapeDtypeStruct((heads, few), F32),
            jax.ShapeDtypeStruct((few, inner), F32),
        )

        def sums(width):
            return [
                pltpu.VMEM((2, n_chip, 2 * few, width), BF16),
                pltpu.VMEM((n_chip, 2 * few, width), BF16),
                pltpu.VMEM((n_y, NZ, 2 * few, width), BF16),
                pltpu.VMEM((n_y, NZ, 2 * few, width), BF16),
                pltpu.VMEM((NZ, 2 * few, width), BF16),
                pltpu.VMEM((NZ, 2 * few, width), BF16),
            ]

        slab = pltpu.VMEM((n_tm, inner // n_tm, N), F32)
        peers = pltpu.VMEM((n_head, quarter, model), BF16)
        results = pl.pallas_call(
            functools.partial(kernel, n_tm, n_head),
            out_shape=out_shape,
            in_specs=[smem] * 3 + [left] * len(arrays),
            out_specs=(vmem,) * 5,
            scratch_shapes=[pltpu.VMEM(a.shape, a.dtype) for a in arrays]
            + [
                pltpu.VMEM((16, model), BF16),
                pltpu.VMEM((heads, 1, N), F32),
                pltpu.VMEM((n_tm, 1, N), F32),
            ]
            + [slab] * 8
            + [
                pltpu.VMEM((inner, N), F32),
                pltpu.VMEM((inner, N), F32),
                pltpu.VMEM((8, rows), F32),
                pltpu.VMEM((n_head, 8, rows), F32),
                peers,
                peers,
                peers,
                peers,
                pltpu.VMEM((8, 2 * inner), F32),
                pltpu.VMEM((8, 2 * inner), F32),
            ]
            + sums(inner)
            + sums(inner + N)
            + [
                pltpu.VMEM((rows + 8, 2 * inner), F32),
                pltpu.VMEM((rows, 2 * inner), F32),
                pltpu.VMEM((rows, 2 * inner), F32),
                pltpu.VMEM((heads, rows, rows), F32),
                pltpu.VMEM((rows, inner), F32),
                pltpu.SemaphoreType.DMA((LOADS,)),
                pltpu.SemaphoreType.DMA((16,)),
                pltpu.SemaphoreType.DMA((16,)),
            ],
            compiler_params=pltpu.CompilerParams(collective_id=0, has_side_effects=True),
        )(step_bias, log_rate, skip_gain, *arrays)
        layer, rows_grad, w_in, w_dt, w_out = pl.pallas_call(
            hand_over,
            out_shape=out_shape,
            in_specs=[vmem] * 5,
            out_specs=(vmem,) * 5,
        )(*results)
        return (layer, rows_grad, w_in.transpose(1, 0, 2), w_dt.T, w_out)

    in_specs = (
        P("tm", None),
        P(None, None, "head"),
        P(None, "head"),
        P("head"),
        P("head"),
        P(None, None, "head"),
        P(None, "head"),
        P("head"),
        P("head"),
        P(None, "head"),
        P("tm", None),
    )
    out_specs = (
        P(("tm", "head"), None),
        P(("tm", "head"), None),
        P("tm", None, "head"),
        P("tm", "head"),
        P("tm", "head"),
    )
    return jax.shard_map(body, mesh=mesh, in_specs=in_specs, out_specs=out_specs, check_vma=False)
```

time: 86.8 us -> 67.1 us (0.77)
  Pallas kernels: 77.5 us -> 66.3 us
  local copies, waits for them, and re-layouts: 8.27 us -> 0 us
    pallas_call x1 -> x2, Pallas kernels: 77.5 us -> 66.3 us  [the longest x1 64.7 us: body(): pl.pallas_call(functools.partial(kernel, n_tm, n_head), out_shape=out_sha...]
    unnamed x15 -> x0, local copies, waits for them, and re-layouts: 7.11 us -> none
    reshape x1 -> x0, local copies, waits for them, and re-layouts: 1.16 us -> none  [body(): in_weight.reshape(model, 3 * inner)]
where the time goes in v2:
time: 67.1 us; the launch traced here: 67 us
  Pallas kernels  66.3 us (99%)
    pallas_call x1, Pallas kernels, body(): pl.pallas_call(functools.partial(kernel, n_tm, n_head), out_shape=out_sha...  64.7 us
    pallas_call x1, Pallas kernels, body(): pl.pallas_call(hand_over, out_shape=out_shape, in_specs=[vmem] * 5, out_s...  1.6 us

profile of v2, /device:TPU:1, one launch (start us, length us, event | category | flops | bytes accessed | tf_op | source)
XLA Modules:
  0.0 67.0 jit_solution(14948144583085451143)
XLA Ops:
  0.6 64.7 %shard_map.146 = (bf16[64,512]{1,0:T(8,128)(2,1)}, f32[64,512]{1,0:T(8,128)}, f32[3,8,256]{2,1,0:T(8,128)}, f32[4,8]{1,0:T(4,128)}, f32[8,256]{1,0:T(8,128)}) custom-call(f32[4]{0:T(128)} %step_bias.1, f32[4]{0:T(128)} %log_rate.1, f32[4]{0:T(128)} %skip_gain.1, bf16[256,512]{1,0:T(8,128)(2,1)} %series_hbm.1, bf16[3,512,256]{2,1,0:T(8,128)(2,1)} %bitcast.5, ...), custom_call_target="tpu_custom_call" | custom-call | tf_op jit(solution)/shard_map/pallas_call | solution.py:613
  65.4 1.6 %shard_map.147 = (bf16[64,512]{1,0:T(8,128)(2,1)}, f32[64,512]{1,0:T(8,128)}, f32[3,8,256]{2,1,0:T(8,128)}, f32[4,8]{1,0:T(4,128)}, f32[8,256]{1,0:T(8,128)}) custom-call(bf16[64,512]{1,0:T(8,128)(2,1)} %get-tuple-element.15.refs_0_, f32[64,512]{1,0:T(8,128)} %get-tuple-element.16.refs_1_, f32[3,8,256]{2,1,0:T(8,128)} %get-tuple-element.17.refs_2_, ...), custom_call_target="tpu_custom_call" | custom-call | tf_op jit(solution)/shard_map/pallas_call | solution.py:651

commit v3 on v2

v3 whole, which is shorter than its diff:
```python
import functools

import jax
import jax.numpy as jnp
from jax import lax
from jax.experimental import pallas as pl
from jax.experimental.pallas import tpu as pltpu
from jax.sharding import PartitionSpec as P

N = 128
KW = 4
E = 1024
EPS = 1e-05
MESH = pl.DeviceIdType.MESH
F32 = jnp.float32
BF16 = jnp.bfloat16

NZ = 8
ROW = 2 * NZ
RIM, DEC, SCAN1, TOTAL1, BACK1, NORM, LAYER, SCAN2, TOTAL2, BACK2 = range(10)
RIM2, RIM3, ROWS, CORE1, ALONG_Y1, ALONG_Z1, CORE2, ALONG_Y2, ALONG_Z2 = range(10, 19)
CORE3, ALONG_Y3, ALONG_Z3 = range(19, 22)
COPIES = 22
LOADS = 8


def bf(v):
    return v.astype(BF16)


def mm(a, b, ca=1, cb=0):
    return lax.dot_general(
        bf(a), bf(b), (((ca,), (cb,)), ((), ())), preferred_element_type=F32
    )


def parts_of(v, count):
    parts = []
    for _ in range(count):
        head = bf(v)
        parts.append(head)
        v = v - head.astype(F32)
    return parts


def mm_left(exact, v, ca=1, cb=0, count=3):
    total = None
    for part in parts_of(v, count):
        term = mm(exact, part, ca, cb)
        total = term if total is None else total + term
    return total


def mm_right(v, exact, ca=1, cb=0, count=3):
    total = None
    for part in parts_of(v, count):
        term = mm(part, exact, ca, cb)
        total = term if total is None else total + term
    return total


def sigmoid(v):
    return 1.0 / (1.0 + jnp.exp(-v))


def softplus(v):
    return jnp.maximum(v, 0.0) + jnp.log1p(jnp.exp(-jnp.abs(v)))


def spread(scalars, shape, width):
    lane = lax.broadcasted_iota(jnp.int32, shape, 1) // width
    out = jnp.zeros(shape, F32)
    for h in range(scalars.shape[0]):
        out = jnp.where(lane == h, scalars[h], out)
    return out


def kernel(
    n_tm,
    n_head,
    step_bias,
    log_rate,
    skip_gain,
    series_hbm,
    w_in_hbm,
    w_dt_hbm,
    conv_w_hbm,
    conv_b_hbm,
    norm_gain_hbm,
    w_out_hbm,
    cot_hbm,
    layer_ref,
    rows_ref,
    w_in_ref,
    w_dt_ref,
    w_out_ref,
    series,
    w_in,
    w_dt,
    conv_w,
    conv_b,
    norm_gain,
    w_out,
    cot,
    rim_in,
    dec_send,
    dec_all,
    state_send,
    state_all,
    total_send,
    total_all,
    prefix_send,
    prefix_all,
    back_send,
    back_all,
    rest_send,
    rest_all,
    suffix_send,
    suffix_all,
    within,
    own_keep,
    norm_send,
    norm_all,
    layer_send,
    layer_all,
    grow_send,
    grow_all,
    rim2_send,
    rim2_in,
    rim3_send,
    rim3_in,
    core1_send,
    core1_in,
    y1_send,
    y1_all,
    z1_send,
    z1_all,
    core2_send,
    core2_in,
    y2_send,
    y2_all,
    z2_send,
    z2_all,
    core3_send,
    core3_in,
    y3_send,
    y3_all,
    z3_send,
    z3_all,
    pre_buf,
    conv_buf,
    act_buf,
    decays,
    inside_buf,
    load_sem,
    send_sem,
    recv_sem,
):
    me = lax.axis_index("tm")
    mine = lax.axis_index("head")
    core = lax.rem(me, 2)
    place = lax.rem(me, ROW)
    at_z = place // 2
    at_y = me // ROW
    n_y = n_tm // ROW
    n_chip = n_tm // 2
    rows, model = series.shape
    inner = w_out.shape[1]
    heads = step_bias.shape[0]
    size = inner // heads
    per_owner = inner // ROW
    owners_per_head = ROW // heads
    quarter = rows // n_head
    few = model // n_tm
    nxt, prv = lax.rem(me + 1, n_tm), lax.rem(me + n_tm - 1, n_tm)

    barrier = pltpu.get_barrier_semaphore()
    far_first = sorted(range(1, ROW), key=lambda d: -min(d, ROW - d))
    across = (2, 1, 3)
    z_first = (4, 3, 5, 2, 6, 1, 7)
    row_peers = [at_y * ROW + lax.rem(place + d, ROW) for d in far_first]
    y_peers = [lax.rem(at_y + d, n_y) for d in across]
    z_peers = [lax.rem(at_z + d, NZ) for d in z_first]
    head_peers = [lax.rem(mine + d, n_head) for d in across]

    def greet(device):
        pl.semaphore_signal(barrier, inc=1, device_id=device, device_id_type=MESH)

    for peer in row_peers:
        greet((peer, mine))
    for peer in y_peers:
        greet((peer * ROW + place, mine))
    for peer in head_peers:
        greet((me, peer))
    greet((nxt, mine))
    greet((prv, mine))
    greeted = len(row_peers) + len(y_peers) + len(head_peers) + 2
    loads = [
        pltpu.make_async_copy(src, dst, load_sem.at[k])
        for k, (src, dst) in enumerate(
            [
                (w_dt_hbm, w_dt),
                (series_hbm, series),
                (w_in_hbm, w_in),
                (conv_w_hbm, conv_w),
                (conv_b_hbm, conv_b),
                (cot_hbm, cot),
                (w_out_hbm, w_out),
                (norm_gain_hbm, norm_gain),
            ]
        )
    ]
    for load in loads:
        load.start()

    def push(src, dst, which, device):
        pltpu.make_async_remote_copy(
            src_ref=src,
            dst_ref=dst,
            send_sem=send_sem.at[which],
            recv_sem=recv_sem.at[which],
            device_id=device,
            device_id_type=MESH,
        ).start()

    def arrived(ref, which):
        pltpu.make_async_copy(ref, ref, recv_sem.at[which]).wait()

    def departed(ref, which):
        pltpu.make_async_copy(ref, ref, send_sem.at[which]).wait()

    def to_row(source_of, dst, which):
        for peer in row_peers:
            at = lax.rem(peer, ROW)
            push(source_of(at), dst.at[place], which, (peer, mine))

    def to_heads(source_of, dst, which):
        for peer in head_peers:
            push(source_of(peer), dst.at[mine], which, (me, peer))

    def to_y(source_of, dst, which):
        for peer in y_peers:
            push(source_of(peer), dst.at[at_y], which, (peer * ROW + place, mine))

    def to_z(source_of, dst, which):
        for peer in z_peers:
            to = at_y * ROW + peer * 2 + core
            push(source_of(peer), dst.at[at_z], which, (to, mine))

    def over(first, everything, at, count):
        total = first
        for d in range(1, count):
            total = total + everything[lax.rem(at + d, count)].astype(F32)
        return total

    def chosen(width, per):
        return (
            lax.broadcasted_iota(jnp.int32, (width, heads), 0) // per
            == lax.broadcasted_iota(jnp.int32, (width, heads), 1)
        ).astype(BF16)

    rate_wide = jnp.exp(spread(log_rate, (1, inner), size))
    skip_wide = spread(skip_gain, (1, inner), size)
    row_id = lax.broadcasted_iota(jnp.int32, (rows, rows), 0)
    col_id = lax.broadcasted_iota(jnp.int32, (rows, rows), 1)
    below = col_id <= row_id
    loads[0].wait()
    w_dt_wide = bf(mm(chosen(inner, size), w_dt[...]))
    w_dt_rows = bf(mm(chosen(N, 1), w_dt[...]))
    loads[1].wait()
    step = softplus(mm(series[...], w_dt_wide, 1, 1) + spread(step_bias, (1, inner), size))
    shift_n = mm(series[...], w_dt_rows, 1, 1) + spread(step_bias, (1, N), 1)
    run = mm_left(below.astype(BF16), -step * rate_wide)
    last = run[rows - 1 : rows, :]
    for h in range(heads):
        dec_send[h] = jnp.broadcast_to(last[:, h * size : h * size + 1], (1, N))
    loads[2].wait()
    pre_buf[pl.ds(0, 8), :] = jnp.zeros((8, 2 * inner), F32)
    pre_buf[pl.ds(8, rows), :inner] = bf(mm(series[...], w_in[1])).astype(F32)
    pre_buf[pl.ds(8, rows), inner:] = bf(mm(series[...], w_in[2])).astype(F32)
    remain = jnp.exp(last - run)
    weight = remain * step

    def conv_row(k):
        return jnp.concatenate([conv_w[k, 0:1, :], conv_w[k, 1:2, :]], axis=1)

    loads[3].wait()
    loads[4].wait()

    def convolve(count):
        conv = jnp.concatenate([conv_b[0:1, :], conv_b[1:2, :]], axis=1)
        for k in range(KW):
            conv = conv + conv_row(k) * pre_buf[pl.ds(8 - (KW - 1) + k, count), :]
        conv_sig = sigmoid(conv)
        conv_buf[pl.ds(0, count), :] = conv_sig * (1.0 + conv * (1.0 - conv_sig))
        active = bf(conv * conv_sig).astype(F32)
        act_buf[pl.ds(0, count), :] = active
        return active

    active = convolve(rows)
    first = 16
    later = lax.broadcasted_iota(jnp.int32, (rows, inner), 0) >= first
    own = mm(jnp.where(later, weight * active[:, :inner], 0.0), active[:, inner : inner + N], 0, 0)

    pl.semaphore_wait(barrier, greeted)
    push(series.at[pl.ds(rows - 16, 16)], rim_in, RIM, (nxt, mine))
    to_row(lambda at: dec_send.at[at // owners_per_head], dec_all, DEC)
    dec_all[place] = dec_send[place // owners_per_head]

    arrived(rim_in, RIM)
    for s in (1, 2):
        rim = bf(mm(rim_in[...], w_in[s])).astype(F32)[8:16]
        pre_buf[pl.ds(0, 8), pl.ds((s - 1) * inner, inner)] = jnp.where(me > 0, rim, 0.0)
    active = convolve(first)
    own = own + mm(weight[:first] * active[:, :inner], active[:, inner : inner + N], 0, 0)

    def exchange(own, send, everything, totals, all_totals, out_send, out_all, which, during):
        scan, total, back = which
        reverse = scan == SCAN2
        slabs = (ROW, per_owner, N)
        send[...] = bf(own).reshape(slabs)
        to_row(lambda at: send.at[at], everything, scan)
        everything[place] = send[place]
        kept = during()
        arrived(everything.at[pl.ds(0, ROW - 1)], scan)
        order = range(ROW - 1, -1, -1) if reverse else range(ROW)
        state = jnp.zeros((per_owner, N), F32)
        log = jnp.zeros((1, N), F32)
        logs = {}
        for k in order:
            within[k] = state
            logs[k] = log
            state = state * jnp.exp(dec_all[k]) + everything[k].astype(F32)
            log = log + dec_all[k]
        totals[pl.ds(0, per_owner), :] = state
        totals[pl.ds(per_owner, 8), :] = jnp.broadcast_to(log, (8, N))
        to_y(lambda peer: totals, all_totals, total)
        all_totals[at_y] = totals[...]
        arrived(all_totals.at[pl.ds(0, n_y - 1)], total)
        outer = jnp.zeros((per_owner, N), F32)
        for k in range(n_y - 1, -1, -1) if reverse else range(n_y):
            new = outer * jnp.exp(all_totals[k, per_owner : per_owner + 1, :])
            new = new + all_totals[k, :per_owner, :]
            outer = jnp.where(k > at_y if reverse else k < at_y, new, outer)
        for k in range(ROW):
            out_send[k] = bf(within[k] + jnp.exp(logs[k]) * outer)
        to_row(lambda at: out_send.at[at], out_all, back)
        out_all[place] = out_send[place]
        return kept

    def collect(out_all, back):
        arrived(out_all.at[pl.ds(0, ROW - 1)], back)
        return out_all[...].reshape(inner, N)

    def by_chip(v, send, lanes):
        v = bf(v).reshape(n_chip, 2, few, v.shape[1])
        for p in range(2):
            send[p, :, :, lanes] = v[:, p]

    def core_stage(send, into, which):
        push(send.at[1 - core], into, which, (me + 1 - 2 * core, mine))

    def y_stage(core_send, core_in, send, everything, which, core_which):
        arrived(core_in, core_which)
        total = core_send[core].astype(F32) + core_in[...].astype(F32)
        send[...] = total.astype(send.dtype).reshape(send.shape)
        to_y(lambda peer: send.at[peer], everything, which)

    def z_stage(y_send, y_all, send, everything, which, y_which):
        arrived(y_all.at[pl.ds(0, n_y - 1)], y_which)
        send[...] = over(y_send[at_y].astype(F32), y_all, at_y, n_y).astype(send.dtype)
        to_z(lambda peer: send.at[peer], everything, which)

    def last_stage(z_send, z_all, which):
        arrived(z_all.at[pl.ds(0, NZ - 1)], which)
        return over(z_send[at_z].astype(F32), z_all, at_z, NZ)

    own_keep[...] = own

    def intra_forward():
        x = bf(act_buf[:, :inner])
        b = bf(act_buf[:, inner : inner + N])
        c = bf(act_buf[:, inner + N :])
        run_t = run.T
        step_t = step.T
        scores = mm(c, b, 1, 1)
        for h in range(heads):
            at = slice(h * size, (h + 1) * size)
            gap = run[:, h * size : h * size + 1] - run_t[h * size : h * size + 1, :]
            decay = jnp.exp(jnp.where(below, gap, -1e30))
            decays[h] = decay
            mixing = scores * decay * step_t[h * size : h * size + 1, :]
            inside_buf[:, at] = mm(mixing, x[:, at])
        gate = bf(mm(series[...], w_in[0])).astype(F32)
        gate_sig = sigmoid(gate)
        for k in (5, 6, 7):
            loads[k].wait()
        gain_grad = norm_gain[...] * mm(cot[...], w_out[...])
        arrived(dec_all.at[pl.ds(0, ROW - 1)], DEC)
        return x, b, c, scores, run_t, step_t, jnp.exp(run), gate, gate_sig, gain_grad

    x, b, c, scores, run_t, step_t, grow, gate, gate_sig, gain_grad = exchange(
        own,
        state_send,
        state_all,
        total_send,
        total_all,
        prefix_send,
        prefix_all,
        (SCAN1, TOTAL1, BACK1),
        intra_forward,
    )
    xw = x.astype(F32)
    gate_act = gate * gate_sig
    start = collect(prefix_all, BACK1)

    ssm = inside_buf[...] + grow * mm(c, start, 1, 1)
    y = ssm + skip_wide * xw
    gated = y * gate_act
    ones = jnp.ones((8, inner), BF16)
    power = mm_left(ones, gated * gated, 1, 1, 2)
    cross = mm_left(ones, gated * gain_grad, 1, 1, 2)
    first_row = lax.broadcasted_iota(jnp.int32, (8, rows), 0) == 0
    norm_send[...] = jnp.where(first_row, power, cross)
    to_heads(lambda peer: norm_send, norm_all, NORM)
    norm_all[mine] = norm_send[...]
    arrived(norm_all.at[pl.ds(0, n_head - 1)], NORM)
    totals = norm_all[0]
    for p in range(1, n_head):
        totals = totals + norm_all[p]
    inv_row = lax.rsqrt(totals[0:1] / E + EPS)
    coef_row = inv_row * inv_row * inv_row * totals[1:2] / E
    inv = jnp.broadcast_to(inv_row, (inner, rows)).T
    coef = jnp.broadcast_to(coef_row, (inner, rows)).T
    grad_gated = inv * gain_grad - gated * coef
    grad_y = grad_gated * gate_act
    gy = bf(grad_y)
    grown = bf(grow * grad_y)

    def unfold(lanes):
        def tap(k):
            return conv_row(k)[:, lanes] * pre_buf[pl.ds(KW - 1 - k, rows), lanes]

        total = tap(0)
        for k in range(1, KW):
            total = total + tap(k)
        return bf(total)

    c_lanes = slice(inner + N, 2 * inner)
    xb_lanes = slice(0, inner + N)
    is_last = me == n_tm - 1

    def intra_backward():
        group = jnp.zeros((rows, rows), F32)
        for h in range(heads):
            at = slice(h * size, (h + 1) * size)
            inside_buf[:, at] = mm(scores * decays[h], gy[:, at], 0, 0)
            group = group + decays[h] * mm(gy[:, at], x[:, at], 1, 1) * (
                step_t[h * size : h * size + 1, :]
            )
        grad_conv = (mm(group, b) + mm(grown, start)) * conv_buf[:, c_lanes]
        pre_buf[pl.ds(0, rows), c_lanes] = grad_conv
        rim3_send[...] = grad_conv[0:8]
        push(rim3_send, rim3_in, RIM3, (prv, mine))
        grad_b = mm(group, c, 0, 0)
        normed = bf(gated * inv * norm_gain[...])
        grad_gate = bf(grad_gated * y * (gate_sig * (1.0 + gate * (1.0 - gate_sig))))
        by_chip(mm(cot[...], normed, 0, 0), core1_send, slice(0, inner))
        by_chip(mm(series[...], grad_gate, 0, 0), core1_send, slice(inner, 2 * inner))
        part = bf(mm(normed, w_out[...], 1, 1))
        for p in range(n_head):
            layer_send[p] = part[p * quarter : (p + 1) * quarter]
        to_heads(lambda peer: layer_send.at[peer], layer_all, LAYER)
        layer_all[mine] = layer_send[mine]
        arrived(rim3_in, RIM3)
        pre_buf[pl.ds(rows, 8), c_lanes] = jnp.where(is_last, 0.0, rim3_in[...])
        grad_pre_c = unfold(c_lanes)
        by_chip(mm(series[...], grad_pre_c, 0, 0), core1_send, slice(2 * inner, 2 * inner + N))
        core_stage(core1_send, core1_in, CORE1)
        return grad_b, grad_gate, grad_pre_c

    grad_b, grad_gate, grad_pre_c = exchange(
        mm(grown, c, 0, 0),
        back_send,
        back_all,
        rest_send,
        rest_all,
        suffix_send,
        suffix_all,
        (SCAN2, TOTAL2, BACK2),
        intra_backward,
    )
    y_stage(core1_send, core1_in, y1_send, y1_all, ALONG_Y1, CORE1)
    after = collect(suffix_all, BACK2)

    back_b = inside_buf[...] + remain * mm(b, after, 1, 1)
    grad_x = skip_wide * grad_y + step * back_b
    grad_b = grad_b + mm(weight * xw, after)
    gc = jnp.concatenate([grad_x, grad_b], axis=1) * conv_buf[:, xb_lanes]
    pre_buf[pl.ds(0, rows), xb_lanes] = gc
    rim2_send[...] = gc[0:8]
    push(rim2_send, rim2_in, RIM2, (prv, mine))

    choose = (
        lax.broadcasted_iota(jnp.int32, (inner, N), 0) // size
        == lax.broadcasted_iota(jnp.int32, (inner, N), 1)
    )
    pick = choose.astype(BF16)
    x_back = mm_right(xw * back_b, pick)
    grad_cum = mm_right(grad_y * ssm, pick) - softplus(shift_n) * x_back
    final = jnp.exp(run_t[:, rows - 1 : rows]) * start.astype(F32) + own_keep[...]
    carried = jnp.sum(
        jnp.where(choose, jnp.sum(after.astype(F32) * final, axis=1, keepdims=True), 0.0),
        axis=0,
        keepdims=True,
    )
    grad_log = mm_left((col_id >= row_id).astype(BF16), grad_cum) + carried
    rate_n = jnp.exp(spread(log_rate, (1, N), 1))
    grad_raw = bf((x_back - rate_n * grad_log) * sigmoid(shift_n))
    thin = mm(series[...], grad_raw, 0, 0).reshape(n_y, NZ, 2, few, N)
    packed = thin[:, 0]
    for z in range(1, NZ):
        packed = packed + pltpu.roll(thin[:, z].reshape(n_y * 2 * few, N), z * ROW, 1).reshape(
            n_y, 2, few, N
        )
    for p in range(2):
        core3_send[p] = packed[:, p]
    core_stage(core3_send, core3_in, CORE3)

    arrived(rim2_in, RIM2)
    pre_buf[pl.ds(rows, 8), xb_lanes] = jnp.where(is_last, 0.0, rim2_in[...])
    grad_pre = unfold(xb_lanes)
    by_chip(mm(series[...], grad_pre, 0, 0), core2_send, slice(None))
    core_stage(core2_send, core2_in, CORE2)
    z_stage(y1_send, y1_all, z1_send, z1_all, ALONG_Z1, ALONG_Y1)

    grad_bc = jnp.concatenate([grad_pre[:, inner:], grad_pre_c], axis=1)
    grad_rows = bf(
        mm(grad_gate, w_in[0], 1, 1)
        + mm(grad_pre[:, :inner], w_in[1], 1, 1)
        + mm(grad_bc, w_in[2], 1, 1)
        + mm(grad_raw, w_dt_rows)
    )
    y_stage(core2_send, core2_in, y2_send, y2_all, ALONG_Y2, CORE2)
    y_stage(core3_send, core3_in, y3_send, y3_all, ALONG_Y3, CORE3)
    for p in range(n_head):
        grow_send[p] = grad_rows[p * quarter : (p + 1) * quarter]
    to_heads(lambda peer: grow_send.at[peer], grow_all, ROWS)
    grow_all[mine] = grow_send[mine]

    def over_heads(everything):
        total = everything[0].astype(F32)
        for p in range(1, n_head):
            total = total + everything[p].astype(F32)
        return total

    arrived(layer_all.at[pl.ds(0, n_head - 1)], LAYER)
    layer_ref[...] = bf(over_heads(layer_all))
    total1 = last_stage(z1_send, z1_all, ALONG_Z1)
    w_out_ref[...] = total1[:, :inner]
    w_in_ref[0] = total1[:, inner : 2 * inner]
    w_in_ref[2, :, N:] = total1[:, 2 * inner :]
    z_stage(y2_send, y2_all, z2_send, z2_all, ALONG_Z2, ALONG_Y2)
    arrived(y3_all.at[pl.ds(0, n_y - 1)], ALONG_Y3)
    z3_send[...] = over(y3_send[at_y], y3_all, at_y, n_y)
    to_z(lambda peer: z3_send, z3_all, ALONG_Z3)
    arrived(grow_all.at[pl.ds(0, n_head - 1)], ROWS)
    rows_ref[...] = over_heads(grow_all)
    total2 = last_stage(z2_send, z2_all, ALONG_Z2)
    w_in_ref[1] = total2[:, :inner]
    w_in_ref[2, :, :N] = total2[:, inner:]
    arrived(z3_all.at[pl.ds(0, NZ - 1)], ALONG_Z3)
    total3 = over(z3_send[...], z3_all, at_z, NZ)
    thin = total3
    for z in range(1, NZ):
        thin = jnp.where(at_z == z, pltpu.roll(total3, N - z * ROW, 1), thin)
    w_dt_ref[...] = thin.T[:heads]

    departed(rim_in, RIM)
    departed(rim2_in, RIM2)
    departed(rim3_in, RIM3)
    for ref, which in (
        (dec_all, DEC),
        (state_all, SCAN1),
        (prefix_all, BACK1),
        (back_all, SCAN2),
        (suffix_all, BACK2),
    ):
        departed(ref.at[pl.ds(0, ROW - 1)], which)
    for ref, which in ((norm_all, NORM), (layer_all, LAYER), (grow_all, ROWS)):
        departed(ref.at[pl.ds(0, n_head - 1)], which)
    for ref, which in (
        (total_all, TOTAL1),
        (rest_all, TOTAL2),
        (y1_all, ALONG_Y1),
        (y2_all, ALONG_Y2),
        (y3_all, ALONG_Y3),
    ):
        departed(ref.at[pl.ds(0, n_y - 1)], which)
    for ref, which in ((z1_all, ALONG_Z1), (z2_all, ALONG_Z2), (z3_all, ALONG_Z3)):
        departed(ref.at[pl.ds(0, NZ - 1)], which)
    departed(core1_in, CORE1)
    departed(core2_in, CORE2)
    departed(core3_in, CORE3)


def hand_over(*refs):
    half = len(refs) // 2
    for src, dst in zip(refs[:half], refs[half:]):
        dst[...] = src[...]


def solution(mesh):
    n_tm, n_head = mesh.shape["tm"], mesh.shape["head"]

    def body(
        series,
        in_weight,
        step_weight,
        step_bias,
        log_rate,
        conv_weight,
        conv_bias,
        skip_gain,
        norm_gain,
        out_weight,
        cotangent,
    ):
        rows, model = series.shape
        inner = out_weight.shape[1]
        heads = step_bias.shape[0]
        few = model // n_tm
        quarter = rows // n_head
        n_chip = n_tm // 2
        n_y = n_tm // ROW
        vmem = pl.BlockSpec(memory_space=pltpu.VMEM)
        smem = pl.BlockSpec(memory_space=pltpu.SMEM)
        left = pl.BlockSpec(memory_space=pl.ANY)
        arrays = (
            series,
            in_weight.transpose(1, 0, 2),
            step_weight.T,
            conv_weight,
            conv_bias,
            norm_gain.reshape(1, inner),
            out_weight,
            cotangent,
        )
        out_shape = (
            jax.ShapeDtypeStruct((quarter, model), BF16),
            jax.ShapeDtypeStruct((quarter, model), F32),
            jax.ShapeDtypeStruct((3, few, inner), F32),
            jax.ShapeDtypeStruct((heads, few), F32),
            jax.ShapeDtypeStruct((few, inner), F32),
        )

        def sums(width):
            return [
                pltpu.VMEM((2, n_chip, few, width), BF16),
                pltpu.VMEM((n_chip, few, width), BF16),
                pltpu.VMEM((n_y, NZ, few, width), BF16),
                pltpu.VMEM((n_y, NZ, few, width), BF16),
                pltpu.VMEM((NZ, few, width), BF16),
                pltpu.VMEM((NZ, few, width), BF16),
            ]

        per_owner = inner // ROW
        slab = pltpu.VMEM((ROW, per_owner, N), BF16)
        scan = [
            slab,
            slab,
            pltpu.VMEM((per_owner + 8, N), F32),
            pltpu.VMEM((n_y, per_owner + 8, N), F32),
            slab,
            slab,
        ]
        peers = pltpu.VMEM((n_head, quarter, model), BF16)
        results = pl.pallas_call(
            functools.partial(kernel, n_tm, n_head),
            out_shape=out_shape,
            in_specs=[smem] * 3 + [left] * len(arrays),
            out_specs=(vmem,) * 5,
            scratch_shapes=[pltpu.VMEM(a.shape, a.dtype) for a in arrays]
            + [
                pltpu.VMEM((16, model), BF16),
                pltpu.VMEM((heads, 1, N), F32),
                pltpu.VMEM((ROW, 1, N), F32),
            ]
            + scan
            + scan
            + [
                pltpu.VMEM((ROW, per_owner, N), F32),
                pltpu.VMEM((inner, N), F32),
                pltpu.VMEM((8, rows), F32),
                pltpu.VMEM((n_head, 8, rows), F32),
                peers,
                peers,
                peers,
                peers,
                pltpu.VMEM((8, inner + N), F32),
                pltpu.VMEM((8, inner + N), F32),
                pltpu.VMEM((8, N), F32),
                pltpu.VMEM((8, N), F32),
            ]
            + sums(2 * inner + N)
            + sums(inner + N)
            + [
                pltpu.VMEM((2, n_y, few, N), F32),
                pltpu.VMEM((n_y, few, N), F32),
                pltpu.VMEM((n_y, few, N), F32),
                pltpu.VMEM((n_y, few, N), F32),
                pltpu.VMEM((few, N), F32),
                pltpu.VMEM((NZ, few, N), F32),
                pltpu.VMEM((rows + 8, 2 * inner), F32),
                pltpu.VMEM((rows, 2 * inner), F32),
                pltpu.VMEM((rows, 2 * inner), F32),
                pltpu.VMEM((heads, rows, rows), F32),
                pltpu.VMEM((rows, inner), F32),
                pltpu.SemaphoreType.DMA((LOADS,)),
                pltpu.SemaphoreType.DMA((COPIES,)),
                pltpu.SemaphoreType.DMA((COPIES,)),
            ],
            compiler_params=pltpu.CompilerParams(collective_id=0, has_side_effects=True),
        )(step_bias, log_rate, skip_gain, *arrays)
        layer, rows_grad, w_in, w_dt, w_out = pl.pallas_call(
            hand_over,
            out_shape=out_shape,
            in_specs=[vmem] * 5,
            out_specs=(vmem,) * 5,
        )(*results)
        return (layer, rows_grad, w_in.transpose(1, 0, 2), w_dt.T, w_out)

    in_specs = (
        P("tm", None),
        P(None, None, "head"),
        P(None, "head"),
        P("head"),
        P("head"),
        P(None, None, "head"),
        P(None, "head"),
        P("head"),
        P("head"),
        P(None, "head"),
        P("tm", None),
    )
    out_specs = (
        P(("tm", "head"), None),
        P(("tm", "head"), None),
        P("tm", None, "head"),
        P("tm", "head"),
        P("tm", "head"),
    )
    return jax.shard_map(body, mesh=mesh, in_specs=in_specs, out_specs=out_specs, check_vma=False)
```

time: 67.1 us -> 61.8 us (0.921)
  Pallas kernels: 66.3 us -> 61.1 us
    pallas_call x1, Pallas kernels: 64.7 us -> 59.5 us  [body(): pl.pallas_call(functools.partial(kernel, n_tm, n_head), out_shape=out_sha...]
where the time goes in v3:
time: 61.8 us; the launch traced here: 61.7 us
  Pallas kernels  61.1 us (99%)
  between operations  0.64 us (1%)
    pallas_call x1, Pallas kernels, body(): pl.pallas_call(functools.partial(kernel, n_tm, n_head), out_shape=out_sha...  59.5 us
    pallas_call x1, Pallas kernels, body(): pl.pallas_call(hand_over, out_shape=out_shape, in_specs=[vmem] * 5, out_s...  1.6 us

profile of v3, /device:TPU:1, one launch (start us, length us, event | category | flops | bytes accessed | tf_op | source)
XLA Modules:
  0.0 61.7 jit_solution(17157065735387550706)
XLA Ops:
  0.6 59.5 %shard_map.146 = (bf16[64,512]{1,0:T(8,128)(2,1)}, f32[64,512]{1,0:T(8,128)}, f32[3,8,256]{2,1,0:T(8,128)}, f32[4,8]{1,0:T(4,128)}, f32[8,256]{1,0:T(8,128)}) custom-call(f32[4]{0:T(128)} %step_bias.1, f32[4]{0:T(128)} %log_rate.1, f32[4]{0:T(128)} %skip_gain.1, bf16[256,512]{1,0:T(8,128)(2,1)} %series_hbm.1, bf16[3,512,256]{2,1,0:T(8,128)(2,1)} %bitcast.5, ...), custom_call_target="tpu_custom_call" | custom-call | tf_op jit(solution)/shard_map/pallas_call | solution.py:678
  60.1 1.6 %shard_map.147 = (bf16[64,512]{1,0:T(8,128)(2,1)}, f32[64,512]{1,0:T(8,128)}, f32[3,8,256]{2,1,0:T(8,128)}, f32[4,8]{1,0:T(4,128)}, f32[8,256]{1,0:T(8,128)}) custom-call(bf16[64,512]{1,0:T(8,128)(2,1)} %get-tuple-element.15.refs_0_, f32[64,512]{1,0:T(8,128)} %get-tuple-element.16.refs_1_, f32[3,8,256]{2,1,0:T(8,128)} %get-tuple-element.17.refs_2_, ...), custom_call_target="tpu_custom_call" | custom-call | tf_op jit(solution)/shard_map/pallas_call | solution.py:725

commit v4 on v3

--- a/solution.py
+++ b/solution.py
@@ -19,9 +19,9 @@
 ROW = 2 * NZ
 RIM, DEC, SCAN1, TOTAL1, BACK1, NORM, LAYER, SCAN2, TOTAL2, BACK2 = range(10)
 RIM2, RIM3, ROWS, CORE1, ALONG_Y1, ALONG_Z1, CORE2, ALONG_Y2, ALONG_Z2 = range(10, 19)
-CORE3, ALONG_Y3, ALONG_Z3 = range(19, 22)
-COPIES = 22
-LOADS = 8
+CORE3, ALONG_Y3, ALONG_Z3, FIRST_Z, THEN_Y = range(19, 24)
+COPIES = 24
+LOADS = 11
 
 
 def bf(v):
@@ -78,9 +78,9 @@
 def kernel(
     n_tm,
     n_head,
-    step_bias,
-    log_rate,
-    skip_gain,
+    step_bias_hbm,
+    log_rate_hbm,
+    skip_gain_hbm,
     series_hbm,
     w_in_hbm,
     w_dt_hbm,
@@ -94,6 +94,9 @@
     w_in_ref,
     w_dt_ref,
     w_out_ref,
+    step_bias,
+    log_rate,
+    skip_gain,
     series,
     w_in,
     w_dt,
@@ -147,6 +150,11 @@
     y3_all,
     z3_send,
     z3_all,
+    zb_send,
+    zb_all,
+    yb_send,
+    yb_all,
+    factors,
     pre_buf,
     conv_buf,
     act_buf,
@@ -174,6 +182,27 @@
     few = model // n_tm
     nxt, prv = lax.rem(me + 1, n_tm), lax.rem(me + n_tm - 1, n_tm)
 
+    loads = [
+        pltpu.make_async_copy(src, dst, load_sem.at[k])
+        for k, (src, dst) in enumerate(
+            [
+                (w_dt_hbm, w_dt),
+                (series_hbm, series),
+                (w_in_hbm, w_in),
+                (conv_w_hbm, conv_w),
+                (conv_b_hbm, conv_b),
+                (step_bias_hbm, step_bias),
+                (log_rate_hbm, log_rate),
+                (skip_gain_hbm, skip_gain),
+                (cot_hbm, cot),
+                (w_out_hbm, w_out),
+                (norm_gain_hbm, norm_gain),
+            ]
+        )
+    ]
+    for load in loads:
+        load.start()
+
     barrier = pltpu.get_barrier_semaphore()
     far_first = sorted(range(1, ROW), key=lambda d: -min(d, ROW - d))
     across = (2, 1, 3)
@@ -195,24 +224,6 @@
     greet((nxt, mine))
     greet((prv, mine))
     greeted = len(row_peers) + len(y_peers) + len(head_peers) + 2
-    loads = [
-        pltpu.make_async_copy(src, dst, load_sem.at[k])
-        for k, (src, dst) in enumerate(
-            [
-                (w_dt_hbm, w_dt),
-                (series_hbm, series),
-                (w_in_hbm, w_in),
-                (conv_w_hbm, conv_w),
-                (conv_b_hbm, conv_b),
-                (cot_hbm, cot),
-                (w_out_hbm, w_out),
-                (norm_gain_hbm, norm_gain),
-            ]
-        )
-    ]
-    for load in loads:
-        load.start()
-
     def push(src, dst, which, device):
         pltpu.make_async_remote_copy(
             src_ref=src,
@@ -259,12 +270,13 @@
             == lax.broadcasted_iota(jnp.int32, (width, heads), 1)
         ).astype(BF16)
 
+    for k in (5, 6, 7, 0):
+        loads[k].wait()
     rate_wide = jnp.exp(spread(log_rate, (1, inner), size))
     skip_wide = spread(skip_gain, (1, inner), size)
     row_id = lax.broadcasted_iota(jnp.int32, (rows, rows), 0)
     col_id = lax.broadcasted_iota(jnp.int32, (rows, rows), 1)
     below = col_id <= row_id
-    loads[0].wait()
     w_dt_wide = bf(mm(chosen(inner, size), w_dt[...]))
     w_dt_rows = bf(mm(chosen(N, 1), w_dt[...]))
     loads[1].wait()
@@ -278,6 +290,11 @@
     pre_buf[pl.ds(0, 8), :] = jnp.zeros((8, 2 * inner), F32)
     pre_buf[pl.ds(8, rows), :inner] = bf(mm(series[...], w_in[1])).astype(F32)
     pre_buf[pl.ds(8, rows), inner:] = bf(mm(series[...], w_in[2])).astype(F32)
+    pl.semaphore_wait(barrier, greeted)
+    push(series.at[pl.ds(rows - 16, 16)], rim_in, RIM, (nxt, mine))
+    to_row(lambda at: dec_send.at[at // owners_per_head], dec_all, DEC)
+    dec_all[place] = dec_send[place // owners_per_head]
+
     remain = jnp.exp(last - run)
     weight = remain * step
 
@@ -301,12 +318,6 @@
     first = 16
     later = lax.broadcasted_iota(jnp.int32, (rows, inner), 0) >= first
     own = mm(jnp.where(later, weight * active[:, :inner], 0.0), active[:, inner : inner + N], 0, 0)
-
-    pl.semaphore_wait(barrier, greeted)
-    push(series.at[pl.ds(rows - 16, 16)], rim_in, RIM, (nxt, mine))
-    to_row(lambda at: dec_send.at[at // owners_per_head], dec_all, DEC)
-    dec_all[place] = dec_send[place // owners_per_head]
-
     arrived(rim_in, RIM)
     for s in (1, 2):
         rim = bf(mm(rim_in[...], w_in[s])).astype(F32)[8:16]
@@ -325,25 +336,21 @@
         arrived(everything.at[pl.ds(0, ROW - 1)], scan)
         order = range(ROW - 1, -1, -1) if reverse else range(ROW)
         state = jnp.zeros((per_owner, N), F32)
-        log = jnp.zeros((1, N), F32)
-        logs = {}
         for k in order:
             within[k] = state
-            logs[k] = log
-            state = state * jnp.exp(dec_all[k]) + everything[k].astype(F32)
-            log = log + dec_all[k]
+            state = state * factors[0, k] + everything[k].astype(F32)
         totals[pl.ds(0, per_owner), :] = state
-        totals[pl.ds(per_owner, 8), :] = jnp.broadcast_to(log, (8, N))
+        totals[pl.ds(per_owner, 8), :] = jnp.broadcast_to(factors[0, ROW], (8, N))
         to_y(lambda peer: totals, all_totals, total)
         all_totals[at_y] = totals[...]
         arrived(all_totals.at[pl.ds(0, n_y - 1)], total)
         outer = jnp.zeros((per_owner, N), F32)
         for k in range(n_y - 1, -1, -1) if reverse else range(n_y):
-            new = outer * jnp.exp(all_totals[k, per_owner : per_owner + 1, :])
+            new = outer * all_totals[k, per_owner : per_owner + 1, :]
             new = new + all_totals[k, :per_owner, :]
             outer = jnp.where(k > at_y if reverse else k < at_y, new, outer)
         for k in range(ROW):
-            out_send[k] = bf(within[k] + jnp.exp(logs[k]) * outer)
+            out_send[k] = bf(within[k] + factors[2 if reverse else 1, k] * outer)
         to_row(lambda at: out_send.at[at], out_all, back)
         out_all[place] = out_send[place]
         return kept
@@ -393,10 +400,18 @@
             inside_buf[:, at] = mm(mixing, x[:, at])
         gate = bf(mm(series[...], w_in[0])).astype(F32)
         gate_sig = sigmoid(gate)
-        for k in (5, 6, 7):
+        for k in (8, 9, 10):
             loads[k].wait()
         gain_grad = norm_gain[...] * mm(cot[...], w_out[...])
         arrived(dec_all.at[pl.ds(0, ROW - 1)], DEC)
+        for row, order in ((1, range(ROW)), (2, range(ROW - 1, -1, -1))):
+            log = jnp.zeros((1, N), F32)
+            for k in order:
+                factors[row, k] = jnp.exp(log)
+                log = log + dec_all[k]
+        factors[0, ROW] = jnp.exp(log)
+        for k in range(ROW):
+            factors[0, k] = jnp.exp(dec_all[k])
         return x, b, c, scores, run_t, step_t, jnp.exp(run), gate, gate_sig, gain_grad
 
     x, b, c, scores, run_t, step_t, grow, gate, gate_sig, gain_grad = exchange(
@@ -437,9 +452,9 @@
     gy = bf(grad_y)
     grown = bf(grow * grad_y)
 
-    def unfold(lanes):
+    def unfold(lanes, at, count):
         def tap(k):
-            return conv_row(k)[:, lanes] * pre_buf[pl.ds(KW - 1 - k, rows), lanes]
+            return conv_row(k)[:, lanes] * pre_buf[pl.ds(at + KW - 1 - k, count), lanes]
 
         total = tap(0)
         for k in range(1, KW):
@@ -474,7 +489,7 @@
         layer_all[mine] = layer_send[mine]
         arrived(rim3_in, RIM3)
         pre_buf[pl.ds(rows, 8), c_lanes] = jnp.where(is_last, 0.0, rim3_in[...])
-        grad_pre_c = unfold(c_lanes)
+        grad_pre_c = unfold(c_lanes, 0, rows)
         by_chip(mm(series[...], grad_pre_c, 0, 0), core1_send, slice(2 * inner, 2 * inner + N))
         core_stage(core1_send, core1_in, CORE1)
         return grad_b, grad_gate, grad_pre_c
@@ -500,6 +515,9 @@
     pre_buf[pl.ds(0, rows), xb_lanes] = gc
     rim2_send[...] = gc[0:8]
     push(rim2_send, rim2_in, RIM2, (prv, mine))
+    main = rows - 16
+    pre_main = unfold(xb_lanes, 0, main)
+    deep = mm(series[:main], pre_main, 0, 0)
 
     choose = (
         lax.broadcasted_iota(jnp.int32, (inner, N), 0) // size
@@ -529,10 +547,12 @@
 
     arrived(rim2_in, RIM2)
     pre_buf[pl.ds(rows, 8), xb_lanes] = jnp.where(is_last, 0.0, rim2_in[...])
-    grad_pre = unfold(xb_lanes)
-    by_chip(mm(series[...], grad_pre, 0, 0), core2_send, slice(None))
+    pre_rest = unfold(xb_lanes, main, 16)
+    by_chip(deep + mm(series[main:], pre_rest, 0, 0), core2_send, slice(None))
     core_stage(core2_send, core2_in, CORE2)
+    y_stage(core3_send, core3_in, y3_send, y3_all, ALONG_Y3, CORE3)
     z_stage(y1_send, y1_all, z1_send, z1_all, ALONG_Z1, ALONG_Y1)
+    grad_pre = jnp.concatenate([pre_main, pre_rest], axis=0)
 
     grad_bc = jnp.concatenate([grad_pre[:, inner:], grad_pre_c], axis=1)
     grad_rows = bf(
@@ -541,8 +561,6 @@
         + mm(grad_bc, w_in[2], 1, 1)
         + mm(grad_raw, w_dt_rows)
     )
-    y_stage(core2_send, core2_in, y2_send, y2_all, ALONG_Y2, CORE2)
-    y_stage(core3_send, core3_in, y3_send, y3_all, ALONG_Y3, CORE3)
     for p in range(n_head):
         grow_send[p] = grad_rows[p * quarter : (p + 1) * quarter]
     to_heads(lambda peer: grow_send.at[peer], grow_all, ROWS)
@@ -554,21 +572,32 @@
             total = total + everything[p].astype(F32)
         return total
 
+    arrived(core2_in, CORE2)
+    pair = core2_send[core].astype(F32) + core2_in[...].astype(F32)
+    y2_send[...] = bf(pair[:, :, :inner]).reshape(y2_send.shape)
+    to_y(lambda peer: y2_send.at[peer], y2_all, ALONG_Y2)
+    thick = bf(pair[:, :, inner:]).reshape(n_y, NZ, few, N)
+    for z in range(NZ):
+        zb_send[z] = thick[:, z]
+    to_z(lambda peer: zb_send.at[peer], zb_all, FIRST_Z)
     arrived(layer_all.at[pl.ds(0, n_head - 1)], LAYER)
     layer_ref[...] = bf(over_heads(layer_all))
+    arrived(y3_all.at[pl.ds(0, n_y - 1)], ALONG_Y3)
+    z3_send[...] = over(y3_send[at_y], y3_all, at_y, n_y)
+    to_z(lambda peer: z3_send, z3_all, ALONG_Z3)
+    z_stage(y2_send, y2_all, z2_send, z2_all, ALONG_Z2, ALONG_Y2)
+    arrived(zb_all.at[pl.ds(0, NZ - 1)], FIRST_Z)
+    yb_send[...] = bf(over(zb_send[at_z].astype(F32), zb_all, at_z, NZ))
+    to_y(lambda peer: yb_send.at[peer], yb_all, THEN_Y)
     total1 = last_stage(z1_send, z1_all, ALONG_Z1)
     w_out_ref[...] = total1[:, :inner]
     w_in_ref[0] = total1[:, inner : 2 * inner]
     w_in_ref[2, :, N:] = total1[:, 2 * inner :]
-    z_stage(y2_send, y2_all, z2_send, z2_all, ALONG_Z2, ALONG_Y2)
-    arrived(y3_all.at[pl.ds(0, n_y - 1)], ALONG_Y3)
-    z3_send[...] = over(y3_send[at_y], y3_all, at_y, n_y)
-    to_z(lambda peer: z3_send, z3_all, ALONG_Z3)
     arrived(grow_all.at[pl.ds(0, n_head - 1)], ROWS)
     rows_ref[...] = over_heads(grow_all)
-    total2 = last_stage(z2_send, z2_all, ALONG_Z2)
-    w_in_ref[1] = total2[:, :inner]
-    w_in_ref[2, :, :N] = total2[:, inner:]
+    arrived(yb_all.at[pl.ds(0, n_y - 1)], THEN_Y)
+    w_in_ref[2, :, :N] = over(yb_send[at_y].astype(F32), yb_all, at_y, n_y)
+    w_in_ref[1] = last_stage(z2_send, z2_all, ALONG_Z2)
     arrived(z3_all.at[pl.ds(0, NZ - 1)], ALONG_Z3)
     total3 = over(z3_send[...], z3_all, at_z, NZ)
     thin = total3
@@ -595,9 +624,15 @@
         (y1_all, ALONG_Y1),
         (y2_all, ALONG_Y2),
         (y3_all, ALONG_Y3),
+        (yb_all, THEN_Y),
     ):
         departed(ref.at[pl.ds(0, n_y - 1)], which)
-    for ref, which in ((z1_all, ALONG_Z1), (z2_all, ALONG_Z2), (z3_all, ALONG_Z3)):
+    for ref, which in (
+        (z1_all, ALONG_Z1),
+        (z2_all, ALONG_Z2),
+        (z3_all, ALONG_Z3),
+        (zb_all, FIRST_Z),
+    ):
         departed(ref.at[pl.ds(0, NZ - 1)], which)
     departed(core1_in, CORE1)
     departed(core2_in, CORE2)
@@ -634,7 +669,6 @@
         n_chip = n_tm // 2
         n_y = n_tm // ROW
         vmem = pl.BlockSpec(memory_space=pltpu.VMEM)
-        smem = pl.BlockSpec(memory_space=pltpu.SMEM)
         left = pl.BlockSpec(memory_space=pl.ANY)
         arrays = (
             series,
@@ -654,14 +688,14 @@
             jax.ShapeDtypeStruct((few, inner), F32),
         )
 
-        def sums(width):
+        def sums(width, first):
             return [
                 pltpu.VMEM((2, n_chip, few, width), BF16),
                 pltpu.VMEM((n_chip, few, width), BF16),
-                pltpu.VMEM((n_y, NZ, few, width), BF16),
-                pltpu.VMEM((n_y, NZ, few, width), BF16),
-                pltpu.VMEM((NZ, few, width), BF16),
-                pltpu.VMEM((NZ, few, width), BF16),
+                pltpu.VMEM((n_y, NZ, few, first), BF16),
+                pltpu.VMEM((n_y, NZ, few, first), BF16),
+                pltpu.VMEM((NZ, few, first), BF16),
+                pltpu.VMEM((NZ, few, first), BF16),
             ]
 
         per_owner = inner // ROW
@@ -678,9 +712,10 @@
         results = pl.pallas_call(
             functools.partial(kernel, n_tm, n_head),
             out_shape=out_shape,
-            in_specs=[smem] * 3 + [left] * len(arrays),
+            in_specs=[left] * (3 + len(arrays)),
             out_specs=(vmem,) * 5,
-            scratch_shapes=[pltpu.VMEM(a.shape, a.dtype) for a in arrays]
+            scratch_shapes=[pltpu.SMEM((heads,), F32)] * 3
+            + [pltpu.VMEM(a.shape, a.dtype) for a in arrays]
             + [
                 pltpu.VMEM((16, model), BF16),
                 pltpu.VMEM((heads, 1, N), F32),
@@ -702,8 +737,8 @@
                 pltpu.VMEM((8, N), F32),
                 pltpu.VMEM((8, N), F32),
             ]
-            + sums(2 * inner + N)
-            + sums(inner + N)
+            + sums(2 * inner + N, 2 * inner + N)
+            + sums(inner + N, inner)
             + [
                 pltpu.VMEM((2, n_y, few, N), F32),
                 pltpu.VMEM((n_y, few, N), F32),
@@ -711,6 +746,11 @@
                 pltpu.VMEM((n_y, few, N), F32),
                 pltpu.VMEM((few, N), F32),
                 pltpu.VMEM((NZ, few, N), F32),
+                pltpu.VMEM((NZ, n_y, few, N), BF16),
+                pltpu.VMEM((NZ, n_y, few, N), BF16),
+                pltpu.VMEM((n_y, few, N), BF16),
+                pltpu.VMEM((n_y, few, N), BF16),
+                pltpu.VMEM((3, ROW + 1, 1, N), F32),
                 pltpu.VMEM((rows + 8, 2 * inner), F32),
                 pltpu.VMEM((rows, 2 * inner), F32),
                 pltpu.VMEM((rows, 2 * inner), F32),

time: 61.8 us -> 59.4 us (0.961)
  Pallas kernels: 61.1 us -> 58.6 us
    pallas_call x1, Pallas kernels: 59.5 us -> 57 us  [body(): pl.pallas_call(functools.partial(kernel, n_tm, n_head), out_shape=out_sha...]
where the time goes in v4:
time: 59.4 us; the launch traced here: 59.2 us
  Pallas kernels  58.6 us (99%)
  between operations  0.64 us (1%)
    pallas_call x1, Pallas kernels, body(): pl.pallas_call(functools.partial(kernel, n_tm, n_head), out_shape=out_sha...  57 us
    pallas_call x1, Pallas kernels, body(): pl.pallas_call(hand_over, out_shape=out_shape, in_specs=[vmem] * 5, out_s...  1.6 us

profile of v4, /device:TPU:1, one launch (start us, length us, event | category | flops | bytes accessed | tf_op | source)
XLA Modules:
  0.0 59.2 jit_solution(701777484981465561)
XLA Ops:
  0.6 57.0 %shard_map.146 = (bf16[64,512]{1,0:T(8,128)(2,1)}, f32[64,512]{1,0:T(8,128)}, f32[3,8,256]{2,1,0:T(8,128)}, f32[4,8]{1,0:T(4,128)}, f32[8,256]{1,0:T(8,128)}) custom-call(f32[4]{0:T(128)} %step_bias_hbm.1, f32[4]{0:T(128)} %log_rate_hbm.1, f32[4]{0:T(128)} %skip_gain_hbm.1, bf16[256,512]{1,0:T(8,128)(2,1)} %series_hbm.1, bf16[3,512,256]{2,1,0:T(8,128)(2,1)} %bitcast.5, ...), custom_call_target="tpu_custom_call" | custom-call | tf_op jit(solution)/shard_map/pallas_call | solution.py:712
  57.6 1.6 %shard_map.147 = (bf16[64,512]{1,0:T(8,128)(2,1)}, f32[64,512]{1,0:T(8,128)}, f32[3,8,256]{2,1,0:T(8,128)}, f32[4,8]{1,0:T(4,128)}, f32[8,256]{1,0:T(8,128)}) custom-call(bf16[64,512]{1,0:T(8,128)(2,1)} %get-tuple-element.15.refs_0_, f32[64,512]{1,0:T(8,128)} %get-tuple-element.16.refs_1_, f32[3,8,256]{2,1,0:T(8,128)} %get-tuple-element.17.refs_2_, ...), custom_call_target="tpu_custom_call" | custom-call | tf_op jit(solution)/shard_map/pallas_call | solution.py:765

commit v5 on v4

--- a/solution.py
+++ b/solution.py
@@ -19,9 +19,10 @@
 ROW = 2 * NZ
 RIM, DEC, SCAN1, TOTAL1, BACK1, NORM, LAYER, SCAN2, TOTAL2, BACK2 = range(10)
 RIM2, RIM3, ROWS, CORE1, ALONG_Y1, ALONG_Z1, CORE2, ALONG_Y2, ALONG_Z2 = range(10, 19)
-CORE3, ALONG_Y3, ALONG_Z3, FIRST_Z, THEN_Y = range(19, 24)
-COPIES = 24
+CORE3, ALONG_Y3, ALONG_Z3, FIRST_Z, THEN_Y, FACTOR, RIM_ROWS = range(19, 26)
+COPIES = 26
 LOADS = 11
+STORES = 7
 
 
 def bf(v):
@@ -89,6 +90,11 @@
     norm_gain_hbm,
     w_out_hbm,
     cot_hbm,
+    layer_out,
+    rows_out,
+    w_in_out,
+    w_dt_out,
+    w_out_out,
     layer_ref,
     rows_ref,
     w_in_ref,
@@ -106,6 +112,8 @@
     w_out,
     cot,
     rim_in,
+    rim_send,
+    rim_pre,
     dec_send,
     dec_all,
     state_send,
@@ -155,12 +163,16 @@
     yb_send,
     yb_all,
     factors,
+    row_factor_send,
+    row_factor,
     pre_buf,
     conv_buf,
     act_buf,
     decays,
     inside_buf,
+    gc_buf,
     load_sem,
+    store_sem,
     send_sem,
     recv_sem,
 ):
@@ -290,8 +302,11 @@
     pre_buf[pl.ds(0, 8), :] = jnp.zeros((8, 2 * inner), F32)
     pre_buf[pl.ds(8, rows), :inner] = bf(mm(series[...], w_in[1])).astype(F32)
     pre_buf[pl.ds(8, rows), inner:] = bf(mm(series[...], w_in[2])).astype(F32)
+    rim_send[...] = bf(pre_buf[pl.ds(rows, 8), :])
+
     pl.semaphore_wait(barrier, greeted)
-    push(series.at[pl.ds(rows - 16, 16)], rim_in, RIM, (nxt, mine))
+    push(rim_send, rim_pre, RIM, (nxt, mine))
+    push(series.at[pl.ds(rows - 16, 16)], rim_in, RIM_ROWS, (nxt, mine))
     to_row(lambda at: dec_send.at[at // owners_per_head], dec_all, DEC)
     dec_all[place] = dec_send[place // owners_per_head]
 
@@ -318,10 +333,8 @@
     first = 16
     later = lax.broadcasted_iota(jnp.int32, (rows, inner), 0) >= first
     own = mm(jnp.where(later, weight * active[:, :inner], 0.0), active[:, inner : inner + N], 0, 0)
-    arrived(rim_in, RIM)
-    for s in (1, 2):
-        rim = bf(mm(rim_in[...], w_in[s])).astype(F32)[8:16]
-        pre_buf[pl.ds(0, 8), pl.ds((s - 1) * inner, inner)] = jnp.where(me > 0, rim, 0.0)
+    arrived(rim_pre, RIM)
+    pre_buf[pl.ds(0, 8), :] = jnp.where(me > 0, rim_pre[...].astype(F32), 0.0)
     active = convolve(first)
     own = own + mm(weight[:first] * active[:, :inner], active[:, inner : inner + N], 0, 0)
 
@@ -339,15 +352,15 @@
         for k in order:
             within[k] = state
             state = state * factors[0, k] + everything[k].astype(F32)
-        totals[pl.ds(0, per_owner), :] = state
-        totals[pl.ds(per_owner, 8), :] = jnp.broadcast_to(factors[0, ROW], (8, N))
+        totals[...] = bf(state)
         to_y(lambda peer: totals, all_totals, total)
         all_totals[at_y] = totals[...]
+        if not reverse:
+            arrived(row_factor.at[pl.ds(0, n_y - 1)], FACTOR)
         arrived(all_totals.at[pl.ds(0, n_y - 1)], total)
         outer = jnp.zeros((per_owner, N), F32)
         for k in range(n_y - 1, -1, -1) if reverse else range(n_y):
-            new = outer * all_totals[k, per_owner : per_owner + 1, :]
-            new = new + all_totals[k, :per_owner, :]
+            new = outer * row_factor[k] + all_totals[k].astype(F32)
             outer = jnp.where(k > at_y if reverse else k < at_y, new, outer)
         for k in range(ROW):
             out_send[k] = bf(within[k] + factors[2 if reverse else 1, k] * outer)
@@ -403,13 +416,16 @@
         for k in (8, 9, 10):
             loads[k].wait()
         gain_grad = norm_gain[...] * mm(cot[...], w_out[...])
+        arrived(rim_in, RIM_ROWS)
         arrived(dec_all.at[pl.ds(0, ROW - 1)], DEC)
         for row, order in ((1, range(ROW)), (2, range(ROW - 1, -1, -1))):
             log = jnp.zeros((1, N), F32)
             for k in order:
                 factors[row, k] = jnp.exp(log)
                 log = log + dec_all[k]
-        factors[0, ROW] = jnp.exp(log)
+        row_factor_send[...] = jnp.exp(log)
+        to_y(lambda peer: row_factor_send, row_factor, FACTOR)
+        row_factor[at_y] = row_factor_send[...]
         for k in range(ROW):
             factors[0, k] = jnp.exp(dec_all[k])
         return x, b, c, scores, run_t, step_t, jnp.exp(run), gate, gate_sig, gain_grad
@@ -433,10 +449,10 @@
     y = ssm + skip_wide * xw
     gated = y * gate_act
     ones = jnp.ones((8, inner), BF16)
-    power = mm_left(ones, gated * gated, 1, 1, 2)
-    cross = mm_left(ones, gated * gain_grad, 1, 1, 2)
-    first_row = lax.broadcasted_iota(jnp.int32, (8, rows), 0) == 0
-    norm_send[...] = jnp.where(first_row, power, cross)
+    power = mm(ones, gated * gated, 1, 1)
+    cross = mm(ones, gated * gain_grad, 1, 1)
+    norm_send[0:1, :] = power[0:1]
+    norm_send[1:2, :] = cross[0:1]
     to_heads(lambda peer: norm_send, norm_all, NORM)
     norm_all[mine] = norm_send[...]
     arrived(norm_all.at[pl.ds(0, n_head - 1)], NORM)
@@ -464,6 +480,13 @@
     c_lanes = slice(inner + N, 2 * inner)
     xb_lanes = slice(0, inner + N)
     is_last = me == n_tm - 1
+
+    choose = (
+        lax.broadcasted_iota(jnp.int32, (inner, N), 0) // size
+        == lax.broadcasted_iota(jnp.int32, (inner, N), 1)
+    )
+    pick = choose.astype(BF16)
+    rate_n = jnp.exp(spread(log_rate, (1, N), 1))
 
     def intra_backward():
         group = jnp.zeros((rows, rows), F32)
@@ -492,9 +515,11 @@
         grad_pre_c = unfold(c_lanes, 0, rows)
         by_chip(mm(series[...], grad_pre_c, 0, 0), core1_send, slice(2 * inner, 2 * inner + N))
         core_stage(core1_send, core1_in, CORE1)
-        return grad_b, grad_gate, grad_pre_c
-
-    grad_b, grad_gate, grad_pre_c = exchange(
+        along_y = mm_right(grad_y * ssm, pick, 1, 0, 2)
+        final = jnp.exp(run_t[:, rows - 1 : rows]) * start.astype(F32) + own_keep[...]
+        return grad_b, grad_gate, grad_pre_c, along_y, softplus(shift_n), sigmoid(shift_n), final
+
+    grad_b, grad_gate, grad_pre_c, along_y, step_n, slope_n, final = exchange(
         mm(grown, c, 0, 0),
         back_send,
         back_all,
@@ -512,29 +537,34 @@
     grad_x = skip_wide * grad_y + step * back_b
     grad_b = grad_b + mm(weight * xw, after)
     gc = jnp.concatenate([grad_x, grad_b], axis=1) * conv_buf[:, xb_lanes]
-    pre_buf[pl.ds(0, rows), xb_lanes] = gc
     rim2_send[...] = gc[0:8]
     push(rim2_send, rim2_in, RIM2, (prv, mine))
-    main = rows - 16
-    pre_main = unfold(xb_lanes, 0, main)
-    deep = mm(series[:main], pre_main, 0, 0)
-
-    choose = (
-        lax.broadcasted_iota(jnp.int32, (inner, N), 0) // size
-        == lax.broadcasted_iota(jnp.int32, (inner, N), 1)
-    )
-    pick = choose.astype(BF16)
-    x_back = mm_right(xw * back_b, pick)
-    grad_cum = mm_right(grad_y * ssm, pick) - softplus(shift_n) * x_back
-    final = jnp.exp(run_t[:, rows - 1 : rows]) * start.astype(F32) + own_keep[...]
+    gc_buf[pl.ds(0, 16), :] = jnp.zeros((16, inner + N), F32)
+    gc_buf[pl.ds(16, rows), :] = gc
+    gc_buf[pl.ds(16 + rows, 8), :] = jnp.zeros((8, inner + N), F32)
+
+    def unfold_own(at, count):
+        total = conv_row(0)[:, xb_lanes] * gc_buf[pl.ds(at + KW - 1, count), :]
+        for k in range(1, KW):
+            tap = conv_row(k)[:, xb_lanes] * gc_buf[pl.ds(at + KW - 1 - k, count), :]
+            total = total + tap
+        return bf(total)
+
+    before = unfold_own(0, 16)
+    before = jnp.where(me > 0, before, jnp.zeros_like(before))
+    pre_own = unfold_own(16, rows)
+    by_chip(mm(series[...], pre_own, 0, 0) + mm(rim_in[...], before, 0, 0), core2_send, slice(None))
+    core_stage(core2_send, core2_in, CORE2)
+
+    x_back = mm_right(xw * back_b, pick, 1, 0, 2)
+    grad_cum = along_y - step_n * x_back
     carried = jnp.sum(
         jnp.where(choose, jnp.sum(after.astype(F32) * final, axis=1, keepdims=True), 0.0),
         axis=0,
         keepdims=True,
     )
-    grad_log = mm_left((col_id >= row_id).astype(BF16), grad_cum) + carried
-    rate_n = jnp.exp(spread(log_rate, (1, N), 1))
-    grad_raw = bf((x_back - rate_n * grad_log) * sigmoid(shift_n))
+    grad_log = mm_left((col_id >= row_id).astype(BF16), grad_cum, 1, 0, 2) + carried
+    grad_raw = bf((x_back - rate_n * grad_log) * slope_n)
     thin = mm(series[...], grad_raw, 0, 0).reshape(n_y, NZ, 2, few, N)
     packed = thin[:, 0]
     for z in range(1, NZ):
@@ -545,15 +575,21 @@
         core3_send[p] = packed[:, p]
     core_stage(core3_send, core3_in, CORE3)
 
+    arrived(core2_in, CORE2)
+    pair = core2_send[core].astype(F32) + core2_in[...].astype(F32)
+    y2_send[...] = bf(pair[:, :, :inner]).reshape(y2_send.shape)
+    to_y(lambda peer: y2_send.at[peer], y2_all, ALONG_Y2)
+    thick = bf(pair[:, :, inner:]).reshape(n_y, NZ, few, N)
+    for z in range(NZ):
+        zb_send[z] = thick[:, z]
+    to_z(lambda peer: zb_send.at[peer], zb_all, FIRST_Z)
+    z_stage(y1_send, y1_all, z1_send, z1_all, ALONG_Z1, ALONG_Y1)
+    y_stage(core3_send, core3_in, y3_send, y3_all, ALONG_Y3, CORE3)
+
     arrived(rim2_in, RIM2)
-    pre_buf[pl.ds(rows, 8), xb_lanes] = jnp.where(is_last, 0.0, rim2_in[...])
-    pre_rest = unfold(xb_lanes, main, 16)
-    by_chip(deep + mm(series[main:], pre_rest, 0, 0), core2_send, slice(None))
-    core_stage(core2_send, core2_in, CORE2)
-    y_stage(core3_send, core3_in, y3_send, y3_all, ALONG_Y3, CORE3)
-    z_stage(y1_send, y1_all, z1_send, z1_all, ALONG_Z1, ALONG_Y1)
-    grad_pre = jnp.concatenate([pre_main, pre_rest], axis=0)
-
+    gc_buf[pl.ds(16 + rows, 8), :] = jnp.where(is_last, 0.0, rim2_in[...])
+    main = rows - 16
+    grad_pre = jnp.concatenate([pre_own[:main], unfold_own(rows, 16)], axis=0)
     grad_bc = jnp.concatenate([grad_pre[:, inner:], grad_pre_c], axis=1)
     grad_rows = bf(
         mm(grad_gate, w_in[0], 1, 1)
@@ -566,46 +602,53 @@
     to_heads(lambda peer: grow_send.at[peer], grow_all, ROWS)
     grow_all[mine] = grow_send[mine]
 
+    stores = []
+
+    def store(src, dst):
+        copy = pltpu.make_async_copy(src, dst, store_sem.at[len(stores)])
+        copy.start()
+        stores.append(copy)
+
     def over_heads(everything):
         total = everything[0].astype(F32)
         for p in range(1, n_head):
             total = total + everything[p].astype(F32)
         return total
 
-    arrived(core2_in, CORE2)
-    pair = core2_send[core].astype(F32) + core2_in[...].astype(F32)
-    y2_send[...] = bf(pair[:, :, :inner]).reshape(y2_send.shape)
-    to_y(lambda peer: y2_send.at[peer], y2_all, ALONG_Y2)
-    thick = bf(pair[:, :, inner:]).reshape(n_y, NZ, few, N)
-    for z in range(NZ):
-        zb_send[z] = thick[:, z]
-    to_z(lambda peer: zb_send.at[peer], zb_all, FIRST_Z)
-    arrived(layer_all.at[pl.ds(0, n_head - 1)], LAYER)
-    layer_ref[...] = bf(over_heads(layer_all))
+    z_stage(y2_send, y2_all, z2_send, z2_all, ALONG_Z2, ALONG_Y2)
     arrived(y3_all.at[pl.ds(0, n_y - 1)], ALONG_Y3)
     z3_send[...] = over(y3_send[at_y], y3_all, at_y, n_y)
     to_z(lambda peer: z3_send, z3_all, ALONG_Z3)
-    z_stage(y2_send, y2_all, z2_send, z2_all, ALONG_Z2, ALONG_Y2)
     arrived(zb_all.at[pl.ds(0, NZ - 1)], FIRST_Z)
     yb_send[...] = bf(over(zb_send[at_z].astype(F32), zb_all, at_z, NZ))
     to_y(lambda peer: yb_send.at[peer], yb_all, THEN_Y)
+    arrived(layer_all.at[pl.ds(0, n_head - 1)], LAYER)
+    layer_ref[...] = bf(over_heads(layer_all))
+    store(layer_ref, layer_out)
     total1 = last_stage(z1_send, z1_all, ALONG_Z1)
     w_out_ref[...] = total1[:, :inner]
     w_in_ref[0] = total1[:, inner : 2 * inner]
+    store(w_out_ref, w_out_out)
+    store(w_in_ref.at[0], w_in_out.at[0])
     w_in_ref[2, :, N:] = total1[:, 2 * inner :]
     arrived(grow_all.at[pl.ds(0, n_head - 1)], ROWS)
     rows_ref[...] = over_heads(grow_all)
-    arrived(yb_all.at[pl.ds(0, n_y - 1)], THEN_Y)
-    w_in_ref[2, :, :N] = over(yb_send[at_y].astype(F32), yb_all, at_y, n_y)
+    store(rows_ref, rows_out)
     w_in_ref[1] = last_stage(z2_send, z2_all, ALONG_Z2)
+    store(w_in_ref.at[1], w_in_out.at[1])
     arrived(z3_all.at[pl.ds(0, NZ - 1)], ALONG_Z3)
     total3 = over(z3_send[...], z3_all, at_z, NZ)
     thin = total3
     for z in range(1, NZ):
         thin = jnp.where(at_z == z, pltpu.roll(total3, N - z * ROW, 1), thin)
     w_dt_ref[...] = thin.T[:heads]
-
-    departed(rim_in, RIM)
+    store(w_dt_ref, w_dt_out)
+    arrived(yb_all.at[pl.ds(0, n_y - 1)], THEN_Y)
+    w_in_ref[2, :, :N] = over(yb_send[at_y].astype(F32), yb_all, at_y, n_y)
+    store(w_in_ref.at[2], w_in_out.at[2])
+
+    departed(rim_pre, RIM)
+    departed(rim_in, RIM_ROWS)
     departed(rim2_in, RIM2)
     departed(rim3_in, RIM3)
     for ref, which in (
@@ -625,6 +668,7 @@
         (y2_all, ALONG_Y2),
         (y3_all, ALONG_Y3),
         (yb_all, THEN_Y),
+        (row_factor, FACTOR),
     ):
         departed(ref.at[pl.ds(0, n_y - 1)], which)
     for ref, which in (
@@ -637,12 +681,21 @@
     departed(core1_in, CORE1)
     departed(core2_in, CORE2)
     departed(core3_in, CORE3)
+    for copy in stores:
+        copy.wait()
 
 
 def hand_over(*refs):
-    half = len(refs) // 2
-    for src, dst in zip(refs[:half], refs[half:]):
-        dst[...] = src[...]
+    given, results, held, sems = refs[:5], refs[5:10], refs[10:15], refs[15]
+    loads = [pltpu.make_async_copy(given[k], held[k], sems.at[0, k]) for k in range(5)]
+    stores = [pltpu.make_async_copy(held[k], results[k], sems.at[1, k]) for k in range(5)]
+    for load in loads:
+        load.start()
+    for load, store in zip(loads, stores):
+        load.wait()
+        store.start()
+    for store in stores:
+        store.wait()
 
 
 def solution(mesh):
@@ -668,7 +721,6 @@
         quarter = rows // n_head
         n_chip = n_tm // 2
         n_y = n_tm // ROW
-        vmem = pl.BlockSpec(memory_space=pltpu.VMEM)
         left = pl.BlockSpec(memory_space=pl.ANY)
         arrays = (
             series,
@@ -703,8 +755,8 @@
         scan = [
             slab,
             slab,
-            pltpu.VMEM((per_owner + 8, N), F32),
-            pltpu.VMEM((n_y, per_owner + 8, N), F32),
+            pltpu.VMEM((per_owner, N), BF16),
+            pltpu.VMEM((n_y, per_owner, N), BF16),
             slab,
             slab,
         ]
@@ -713,11 +765,14 @@
             functools.partial(kernel, n_tm, n_head),
             out_shape=out_shape,
             in_specs=[left] * (3 + len(arrays)),
-            out_specs=(vmem,) * 5,
-            scratch_shapes=[pltpu.SMEM((heads,), F32)] * 3
+            out_specs=(left,) * 5,
+            scratch_shapes=[pltpu.VMEM(o.shape, o.dtype) for o in out_shape]
+            + [pltpu.SMEM((heads,), F32)] * 3
             + [pltpu.VMEM(a.shape, a.dtype) for a in arrays]
             + [
                 pltpu.VMEM((16, model), BF16),
+                pltpu.VMEM((8, 2 * inner), BF16),
+                pltpu.VMEM((8, 2 * inner), BF16),
                 pltpu.VMEM((heads, 1, N), F32),
                 pltpu.VMEM((ROW, 1, N), F32),
             ]
@@ -726,8 +781,8 @@
             + [
                 pltpu.VMEM((ROW, per_owner, N), F32),
                 pltpu.VMEM((inner, N), F32),
-                pltpu.VMEM((8, rows), F32),
-                pltpu.VMEM((n_head, 8, rows), F32),
+                pltpu.VMEM((2, rows), F32),
+                pltpu.VMEM((n_head, 2, rows), F32),
                 peers,
                 peers,
                 peers,
@@ -750,13 +805,17 @@
                 pltpu.VMEM((NZ, n_y, few, N), BF16),
                 pltpu.VMEM((n_y, few, N), BF16),
                 pltpu.VMEM((n_y, few, N), BF16),
-                pltpu.VMEM((3, ROW + 1, 1, N), F32),
+                pltpu.VMEM((3, ROW, 1, N), F32),
+                pltpu.VMEM((1, N), F32),
+                pltpu.VMEM((n_y, 1, N), F32),
                 pltpu.VMEM((rows + 8, 2 * inner), F32),
                 pltpu.VMEM((rows, 2 * inner), F32),
                 pltpu.VMEM((rows, 2 * inner), F32),
                 pltpu.VMEM((heads, rows, rows), F32),
                 pltpu.VMEM((rows, inner), F32),
+                pltpu.VMEM((rows + 24, inner + N), F32),
                 pltpu.SemaphoreType.DMA((LOADS,)),
+                pltpu.SemaphoreType.DMA((STORES,)),
                 pltpu.SemaphoreType.DMA((COPIES,)),
                 pltpu.SemaphoreType.DMA((COPIES,)),
             ],
@@ -765,8 +824,10 @@
         layer, rows_grad, w_in, w_dt, w_out = pl.pallas_call(
             hand_over,
             out_shape=out_shape,
-            in_specs=[vmem] * 5,
-            out_specs=(vmem,) * 5,
+            in_specs=[left] * 5,
+            out_specs=(left,) * 5,
+            scratch_shapes=[pltpu.VMEM(o.shape, o.dtype) for o in out_shape]
+            + [pltpu.SemaphoreType.DMA((2, 5))],
         )(*results)
         return (layer, rows_grad, w_in.transpose(1, 0, 2), w_dt.T, w_out)
 

time: 59.4 us -> 57.1 us (0.961)
  Pallas kernels: 58.6 us -> 56.4 us
    pallas_call x1, Pallas kernels: 57 us -> 54.7 us  [body(): pl.pallas_call(functools.partial(kernel, n_tm, n_head), out_shape=out_sha...]
where the time goes in v5:
time: 57.1 us; the launch traced here: 57 us
  Pallas kernels  56.4 us (99%)
  between operations  0.64 us (1%)
    pallas_call x1, Pallas kernels, body(): pl.pallas_call(functools.partial(kernel, n_tm, n_head), out_shape=out_sha...  54.7 us
    pallas_call x1, Pallas kernels, body(): pl.pallas_call(hand_over, out_shape=out_shape, in_specs=[left] * 5, out_s...  1.69 us

profile of v5, /device:TPU:1, one launch (start us, length us, event | category | flops | bytes accessed | tf_op | source)
XLA Modules:
  0.0 57.0 jit_solution(17661759969755412502)
XLA Ops:
  0.6 54.7 %shard_map.146 = (bf16[64,512]{1,0:T(8,128)(2,1)}, f32[64,512]{1,0:T(8,128)}, f32[3,8,256]{2,1,0:T(8,128)}, f32[4,8]{1,0:T(4,128)}, f32[8,256]{1,0:T(8,128)}) custom-call(f32[4]{0:T(128)} %step_bias_hbm.1, f32[4]{0:T(128)} %log_rate_hbm.1, f32[4]{0:T(128)} %skip_gain_hbm.1, bf16[256,512]{1,0:T(8,128)(2,1)} %series_hbm.1, bf16[3,512,256]{2,1,0:T(8,128)(2,1)} %bitcast.5, ...), custom_call_target="tpu_custom_call" | custom-call | tf_op jit(solution)/shard_map/pallas_call | solution.py:764
  55.3 1.7 %shard_map.147 = (bf16[64,512]{1,0:T(8,128)(2,1)}, f32[64,512]{1,0:T(8,128)}, f32[3,8,256]{2,1,0:T(8,128)}, f32[4,8]{1,0:T(4,128)}, f32[8,256]{1,0:T(8,128)}) custom-call(bf16[64,512]{1,0:T(8,128)(2,1)} %get-tuple-element.15.refs_0_, f32[64,512]{1,0:T(8,128)} %get-tuple-element.16.refs_1_, f32[3,8,256]{2,1,0:T(8,128)} %get-tuple-element.17.refs_2_, ...), custom_call_target="tpu_custom_call" | custom-call | tf_op jit(solution)/shard_map/pallas_call | solution.py:824

commit v6 on v5

--- a/solution.py
+++ b/solution.py
@@ -19,10 +19,12 @@
 ROW = 2 * NZ
 RIM, DEC, SCAN1, TOTAL1, BACK1, NORM, LAYER, SCAN2, TOTAL2, BACK2 = range(10)
 RIM2, RIM3, ROWS, CORE1, ALONG_Y1, ALONG_Z1, CORE2, ALONG_Y2, ALONG_Z2 = range(10, 19)
-CORE3, ALONG_Y3, ALONG_Z3, FIRST_Z, THEN_Y, FACTOR, RIM_ROWS = range(19, 26)
-COPIES = 26
-LOADS = 11
-STORES = 7
+CORE3, ALONG_Y3, ALONG_Z3, FIRST_Z, THEN_Y, FACTOR, RIM_ROWS, ALONG_Y4, ALONG_Z4 = range(19, 28)
+COPIES = 28
+LOADS = 6
+BIAS, RATE, SKIP, GAIN, CONV_B = range(5)
+W_DT = CONV_B + 2
+GRANT = 56200000
 
 
 def bf(v):
@@ -68,47 +70,32 @@
     return jnp.maximum(v, 0.0) + jnp.log1p(jnp.exp(-jnp.abs(v)))
 
 
-def spread(scalars, shape, width):
+def spread(row, heads, shape, width):
     lane = lax.broadcasted_iota(jnp.int32, shape, 1) // width
     out = jnp.zeros(shape, F32)
-    for h in range(scalars.shape[0]):
-        out = jnp.where(lane == h, scalars[h], out)
+    for h in range(heads):
+        out = jnp.where(lane == h, row[:, h : h + 1], out)
     return out
 
 
 def kernel(
     n_tm,
     n_head,
-    step_bias_hbm,
-    log_rate_hbm,
-    skip_gain_hbm,
+    small_hbm,
     series_hbm,
     w_in_hbm,
-    w_dt_hbm,
     conv_w_hbm,
-    conv_b_hbm,
-    norm_gain_hbm,
     w_out_hbm,
     cot_hbm,
-    layer_out,
-    rows_out,
-    w_in_out,
-    w_dt_out,
-    w_out_out,
     layer_ref,
     rows_ref,
     w_in_ref,
     w_dt_ref,
     w_out_ref,
-    step_bias,
-    log_rate,
-    skip_gain,
+    small,
     series,
     w_in,
-    w_dt,
     conv_w,
-    conv_b,
-    norm_gain,
     w_out,
     cot,
     rim_in,
@@ -152,6 +139,10 @@
     y2_all,
     z2_send,
     z2_all,
+    y4_send,
+    y4_all,
+    z4_send,
+    z4_all,
     core3_send,
     core3_in,
     y3_send,
@@ -172,7 +163,6 @@
     inside_buf,
     gc_buf,
     load_sem,
-    store_sem,
     send_sem,
     recv_sem,
 ):
@@ -186,7 +176,7 @@
     n_chip = n_tm // 2
     rows, model = series.shape
     inner = w_out.shape[1]
-    heads = step_bias.shape[0]
+    heads = w_dt_ref.shape[0]
     size = inner // heads
     per_owner = inner // ROW
     owners_per_head = ROW // heads
@@ -198,17 +188,12 @@
         pltpu.make_async_copy(src, dst, load_sem.at[k])
         for k, (src, dst) in enumerate(
             [
-                (w_dt_hbm, w_dt),
+                (small_hbm, small),
                 (series_hbm, series),
                 (w_in_hbm, w_in),
                 (conv_w_hbm, conv_w),
-                (conv_b_hbm, conv_b),
-                (step_bias_hbm, step_bias),
-                (log_rate_hbm, log_rate),
-                (skip_gain_hbm, skip_gain),
                 (cot_hbm, cot),
                 (w_out_hbm, w_out),
-                (norm_gain_hbm, norm_gain),
             ]
         )
     ]
@@ -282,18 +267,19 @@
             == lax.broadcasted_iota(jnp.int32, (width, heads), 1)
         ).astype(BF16)
 
-    for k in (5, 6, 7, 0):
+    for k in (0, 3):
         loads[k].wait()
-    rate_wide = jnp.exp(spread(log_rate, (1, inner), size))
-    skip_wide = spread(skip_gain, (1, inner), size)
+    rate_wide = jnp.exp(spread(small[RATE : RATE + 1, :N], heads, (1, inner), size))
+    skip_wide = spread(small[SKIP : SKIP + 1, :N], heads, (1, inner), size)
     row_id = lax.broadcasted_iota(jnp.int32, (rows, rows), 0)
     col_id = lax.broadcasted_iota(jnp.int32, (rows, rows), 1)
     below = col_id <= row_id
-    w_dt_wide = bf(mm(chosen(inner, size), w_dt[...]))
-    w_dt_rows = bf(mm(chosen(N, 1), w_dt[...]))
+    w_dt = small[W_DT : W_DT + heads, :]
+    w_dt_wide = bf(mm(chosen(inner, size), w_dt))
+    w_dt_rows = bf(mm(chosen(N, 1), w_dt))
     loads[1].wait()
-    step = softplus(mm(series[...], w_dt_wide, 1, 1) + spread(step_bias, (1, inner), size))
-    shift_n = mm(series[...], w_dt_rows, 1, 1) + spread(step_bias, (1, N), 1)
+    step = softplus(mm(series[...], w_dt_wide, 1, 1) + spread(small[BIAS : BIAS + 1, :N], heads, (1, inner), size))
+    shift_n = mm(series[...], w_dt_rows, 1, 1) + spread(small[BIAS : BIAS + 1, :N], heads, (1, N), 1)
     run = mm_left(below.astype(BF16), -step * rate_wide)
     last = run[rows - 1 : rows, :]
     for h in range(heads):
@@ -314,13 +300,11 @@
     weight = remain * step
 
     def conv_row(k):
-        return jnp.concatenate([conv_w[k, 0:1, :], conv_w[k, 1:2, :]], axis=1)
-
-    loads[3].wait()
-    loads[4].wait()
+        return jnp.concatenate([conv_w[0, k, 0:1, :], conv_w[0, k, 1:2, :]], axis=1)
+
 
     def convolve(count):
-        conv = jnp.concatenate([conv_b[0:1, :], conv_b[1:2, :]], axis=1)
+        conv = jnp.concatenate([small[CONV_B : CONV_B + 1, :inner], small[CONV_B + 1 : CONV_B + 2, :inner]], axis=1)
         for k in range(KW):
             conv = conv + conv_row(k) * pre_buf[pl.ds(8 - (KW - 1) + k, count), :]
         conv_sig = sigmoid(conv)
@@ -347,14 +331,18 @@
         everything[place] = send[place]
         kept = during()
         arrived(everything.at[pl.ds(0, ROW - 1)], scan)
-        order = range(ROW - 1, -1, -1) if reverse else range(ROW)
+        terms = [
+            factors[1 if reverse else 2, k] * everything[k].astype(F32) for k in range(ROW)
+        ]
+        while len(terms) > 1:
+            terms = [terms[k] + terms[k + 1] for k in range(0, len(terms), 2)]
+        totals[...] = bf(terms[0])
+        to_y(lambda peer: totals, all_totals, total)
+        all_totals[at_y] = totals[...]
         state = jnp.zeros((per_owner, N), F32)
-        for k in order:
+        for k in range(ROW - 1, -1, -1) if reverse else range(ROW):
             within[k] = state
             state = state * factors[0, k] + everything[k].astype(F32)
-        totals[...] = bf(state)
-        to_y(lambda peer: totals, all_totals, total)
-        all_totals[at_y] = totals[...]
         if not reverse:
             arrived(row_factor.at[pl.ds(0, n_y - 1)], FACTOR)
         arrived(all_totals.at[pl.ds(0, n_y - 1)], total)
@@ -362,10 +350,14 @@
         for k in range(n_y - 1, -1, -1) if reverse else range(n_y):
             new = outer * row_factor[k] + all_totals[k].astype(F32)
             outer = jnp.where(k > at_y if reverse else k < at_y, new, outer)
-        for k in range(ROW):
-            out_send[k] = bf(within[k] + factors[2 if reverse else 1, k] * outer)
-        to_row(lambda at: out_send.at[at], out_all, back)
-        out_all[place] = out_send[place]
+        def finished(at):
+            return bf(within[at] + factors[2 if reverse else 1, at] * outer)
+
+        for peer in row_peers:
+            at = lax.rem(peer, ROW)
+            out_send[at] = finished(at)
+            push(out_send.at[at], out_all.at[place], back, (peer, mine))
+        out_all[place] = finished(place)
         return kept
 
     def collect(out_all, back):
@@ -413,9 +405,9 @@
             inside_buf[:, at] = mm(mixing, x[:, at])
         gate = bf(mm(series[...], w_in[0])).astype(F32)
         gate_sig = sigmoid(gate)
-        for k in (8, 9, 10):
+        for k in (4, 5):
             loads[k].wait()
-        gain_grad = norm_gain[...] * mm(cot[...], w_out[...])
+        gain_grad = small[GAIN : GAIN + 1, :inner] * mm(cot[...], w_out[...])
         arrived(rim_in, RIM_ROWS)
         arrived(dec_all.at[pl.ds(0, ROW - 1)], DEC)
         for row, order in ((1, range(ROW)), (2, range(ROW - 1, -1, -1))):
@@ -486,7 +478,7 @@
         == lax.broadcasted_iota(jnp.int32, (inner, N), 1)
     )
     pick = choose.astype(BF16)
-    rate_n = jnp.exp(spread(log_rate, (1, N), 1))
+    rate_n = jnp.exp(spread(small[RATE : RATE + 1, :N], heads, (1, N), 1))
 
     def intra_backward():
         group = jnp.zeros((rows, rows), F32)
@@ -501,7 +493,7 @@
         rim3_send[...] = grad_conv[0:8]
         push(rim3_send, rim3_in, RIM3, (prv, mine))
         grad_b = mm(group, c, 0, 0)
-        normed = bf(gated * inv * norm_gain[...])
+        normed = bf(gated * inv * small[GAIN : GAIN + 1, :inner])
         grad_gate = bf(grad_gated * y * (gate_sig * (1.0 + gate * (1.0 - gate_sig))))
         by_chip(mm(cot[...], normed, 0, 0), core1_send, slice(0, inner))
         by_chip(mm(series[...], grad_gate, 0, 0), core1_send, slice(inner, 2 * inner))
@@ -577,8 +569,11 @@
 
     arrived(core2_in, CORE2)
     pair = core2_send[core].astype(F32) + core2_in[...].astype(F32)
-    y2_send[...] = bf(pair[:, :, :inner]).reshape(y2_send.shape)
+    half = inner // 2
+    y2_send[...] = bf(pair[:, :, :half]).reshape(y2_send.shape)
     to_y(lambda peer: y2_send.at[peer], y2_all, ALONG_Y2)
+    y4_send[...] = bf(pair[:, :, half:inner]).reshape(y4_send.shape)
+    to_y(lambda peer: y4_send.at[peer], y4_all, ALONG_Y4)
     thick = bf(pair[:, :, inner:]).reshape(n_y, NZ, few, N)
     for z in range(NZ):
         zb_send[z] = thick[:, z]
@@ -602,13 +597,6 @@
     to_heads(lambda peer: grow_send.at[peer], grow_all, ROWS)
     grow_all[mine] = grow_send[mine]
 
-    stores = []
-
-    def store(src, dst):
-        copy = pltpu.make_async_copy(src, dst, store_sem.at[len(stores)])
-        copy.start()
-        stores.append(copy)
-
     def over_heads(everything):
         total = everything[0].astype(F32)
         for p in range(1, n_head):
@@ -616,6 +604,7 @@
         return total
 
     z_stage(y2_send, y2_all, z2_send, z2_all, ALONG_Z2, ALONG_Y2)
+    z_stage(y4_send, y4_all, z4_send, z4_all, ALONG_Z4, ALONG_Y4)
     arrived(y3_all.at[pl.ds(0, n_y - 1)], ALONG_Y3)
     z3_send[...] = over(y3_send[at_y], y3_all, at_y, n_y)
     to_z(lambda peer: z3_send, z3_all, ALONG_Z3)
@@ -624,28 +613,22 @@
     to_y(lambda peer: yb_send.at[peer], yb_all, THEN_Y)
     arrived(layer_all.at[pl.ds(0, n_head - 1)], LAYER)
     layer_ref[...] = bf(over_heads(layer_all))
-    store(layer_ref, layer_out)
     total1 = last_stage(z1_send, z1_all, ALONG_Z1)
     w_out_ref[...] = total1[:, :inner]
     w_in_ref[0] = total1[:, inner : 2 * inner]
-    store(w_out_ref, w_out_out)
-    store(w_in_ref.at[0], w_in_out.at[0])
     w_in_ref[2, :, N:] = total1[:, 2 * inner :]
     arrived(grow_all.at[pl.ds(0, n_head - 1)], ROWS)
     rows_ref[...] = over_heads(grow_all)
-    store(rows_ref, rows_out)
-    w_in_ref[1] = last_stage(z2_send, z2_all, ALONG_Z2)
-    store(w_in_ref.at[1], w_in_out.at[1])
+    w_in_ref[1, :, :half] = last_stage(z2_send, z2_all, ALONG_Z2)
+    w_in_ref[1, :, half:] = last_stage(z4_send, z4_all, ALONG_Z4)
     arrived(z3_all.at[pl.ds(0, NZ - 1)], ALONG_Z3)
     total3 = over(z3_send[...], z3_all, at_z, NZ)
     thin = total3
     for z in range(1, NZ):
         thin = jnp.where(at_z == z, pltpu.roll(total3, N - z * ROW, 1), thin)
     w_dt_ref[...] = thin.T[:heads]
-    store(w_dt_ref, w_dt_out)
     arrived(yb_all.at[pl.ds(0, n_y - 1)], THEN_Y)
     w_in_ref[2, :, :N] = over(yb_send[at_y].astype(F32), yb_all, at_y, n_y)
-    store(w_in_ref.at[2], w_in_out.at[2])
 
     departed(rim_pre, RIM)
     departed(rim_in, RIM_ROWS)
@@ -667,6 +650,7 @@
         (y1_all, ALONG_Y1),
         (y2_all, ALONG_Y2),
         (y3_all, ALONG_Y3),
+        (y4_all, ALONG_Y4),
         (yb_all, THEN_Y),
         (row_factor, FACTOR),
     ):
@@ -675,24 +659,19 @@
         (z1_all, ALONG_Z1),
         (z2_all, ALONG_Z2),
         (z3_all, ALONG_Z3),
+        (z4_all, ALONG_Z4),
         (zb_all, FIRST_Z),
     ):
         departed(ref.at[pl.ds(0, NZ - 1)], which)
     departed(core1_in, CORE1)
     departed(core2_in, CORE2)
     departed(core3_in, CORE3)
-    for copy in stores:
-        copy.wait()
 
 
 def hand_over(*refs):
-    given, results, held, sems = refs[:5], refs[5:10], refs[10:15], refs[15]
-    loads = [pltpu.make_async_copy(given[k], held[k], sems.at[0, k]) for k in range(5)]
-    stores = [pltpu.make_async_copy(held[k], results[k], sems.at[1, k]) for k in range(5)]
-    for load in loads:
-        load.start()
-    for load, store in zip(loads, stores):
-        load.wait()
+    given, results, sems = refs[:5], refs[5:10], refs[10]
+    stores = [pltpu.make_async_copy(given[k], results[k], sems.at[k]) for k in range(5)]
+    for store in stores:
         store.start()
     for store in stores:
         store.wait()
@@ -721,14 +700,20 @@
         quarter = rows // n_head
         n_chip = n_tm // 2
         n_y = n_tm // ROW
+        vmem = pl.BlockSpec(memory_space=pltpu.VMEM)
         left = pl.BlockSpec(memory_space=pl.ANY)
+        pieces = [v[None] for v in (step_bias, log_rate, skip_gain, norm_gain)] + [conv_bias]
+        pieces.append(step_weight.T.astype(F32))
+        height, at = sum(p.shape[0] for p in pieces), 0
+        few_rows = jnp.zeros((height, model), F32)
+        for p in pieces:
+            below = height - at - p.shape[0]
+            few_rows = few_rows + jnp.pad(p, ((at, below), (0, model - p.shape[1])))
+            at += p.shape[0]
         arrays = (
             series,
             in_weight.transpose(1, 0, 2),
-            step_weight.T,
-            conv_weight,
-            conv_bias,
-            norm_gain.reshape(1, inner),
+            conv_weight[None],
             out_weight,
             cotangent,
         )
@@ -764,10 +749,9 @@
         results = pl.pallas_call(
             functools.partial(kernel, n_tm, n_head),
             out_shape=out_shape,
-            in_specs=[left] * (3 + len(arrays)),
-            out_specs=(left,) * 5,
-            scratch_shapes=[pltpu.VMEM(o.shape, o.dtype) for o in out_shape]
-            + [pltpu.SMEM((heads,), F32)] * 3
+            in_specs=[left] * (1 + len(arrays)),
+            out_specs=(vmem,) * 5,
+            scratch_shapes=[pltpu.VMEM(few_rows.shape, F32)]
             + [pltpu.VMEM(a.shape, a.dtype) for a in arrays]
             + [
                 pltpu.VMEM((16, model), BF16),
@@ -793,7 +777,8 @@
                 pltpu.VMEM((8, N), F32),
             ]
             + sums(2 * inner + N, 2 * inner + N)
-            + sums(inner + N, inner)
+            + sums(inner + N, inner // 2)
+            + sums(inner + N, inner // 2)[2:]
             + [
                 pltpu.VMEM((2, n_y, few, N), F32),
                 pltpu.VMEM((n_y, few, N), F32),
@@ -815,19 +800,18 @@
                 pltpu.VMEM((rows, inner), F32),
                 pltpu.VMEM((rows + 24, inner + N), F32),
                 pltpu.SemaphoreType.DMA((LOADS,)),
-                pltpu.SemaphoreType.DMA((STORES,)),
                 pltpu.SemaphoreType.DMA((COPIES,)),
                 pltpu.SemaphoreType.DMA((COPIES,)),
             ],
-            compiler_params=pltpu.CompilerParams(collective_id=0, has_side_effects=True),
-        )(step_bias, log_rate, skip_gain, *arrays)
+            compiler_params=pltpu.CompilerParams(collective_id=0, has_side_effects=True, vmem_limit_bytes=GRANT),
+        )(few_rows, *arrays)
         layer, rows_grad, w_in, w_dt, w_out = pl.pallas_call(
             hand_over,
             out_shape=out_shape,
-            in_specs=[left] * 5,
+            in_specs=[vmem] * 5,
             out_specs=(left,) * 5,
-            scratch_shapes=[pltpu.VMEM(o.shape, o.dtype) for o in out_shape]
-            + [pltpu.SemaphoreType.DMA((2, 5))],
+            scratch_shapes=[pltpu.SemaphoreType.DMA((5,))],
+            compiler_params=pltpu.CompilerParams(vmem_limit_bytes=1024 * 1024),
         )(*results)
         return (layer, rows_grad, w_in.transpose(1, 0, 2), w_dt.T, w_out)
 

time: 57.1 us -> 56.9 us (level)
  Pallas kernels: 56.4 us -> 54.6 us
  local copies, waits for them, and re-layouts: 0 us -> 1.37 us
    unnamed x0 -> x14, local copies, waits for them, and re-layouts: none -> 1.37 us
    pallas_call x1, Pallas kernels: 1.69 us -> 0.73 us  [body(): pl.pallas_call(hand_over, out_shape=out_shape, in_specs=[vmem] * 5, out_s...]
    pallas_call x1, Pallas kernels: 54.7 us -> 53.9 us  [body(): pl.pallas_call(functools.partial(kernel, n_tm, n_head), out_shape=out_sha...]
where the time goes in v6:
time: 56.9 us; the launch traced here: 56.7 us
  Pallas kernels  54.6 us (96%)
  local copies, waits for them, and re-layouts  1.37 us (2%)
  between operations  0.7 us (1%)
    pallas_call x1, Pallas kernels, body(): pl.pallas_call(functools.partial(kernel, n_tm, n_head), out_shape=out_sha...  53.9 us
    unnamed x14, local copies, waits for them, and re-layouts  1.37 us

profile of v6, /device:TPU:1, one launch (start us, length us, event | category | flops | bytes accessed | tf_op | source)
XLA Modules:
  0.0 56.7 jit_solution(14910779587780782661)
XLA Ops:
  0.6 0.0 copy-start.5
  0.6 0.0 copy-start.6
  0.7 0.0 copy-start.1
  0.7 0.0 copy-start.2
  0.7 0.0 copy-start.3
  0.7 0.0 copy-start.4
  0.7 0.6 %copy-done.5 = f32[4]{0:T(128)S(1)} copy-done((f32[4]{0:T(128)S(1)}, f32[4]{0:T(128)}, u32[]{:S(2)}) %copy-start.5) | copy-done | bytes 40
  1.3 0.0 copy-done.6
  1.3 0.0 copy-done.1
  1.4 0.0 copy-done.2
  1.4 0.0 copy-done.3
  1.4 0.0 copy-done.4
  1.4 0.0 copy-start
  1.4 0.7 %copy-done = f32[4,2,256]{2,1,0:T(2,128)S(1)} copy-done((f32[4,2,256]{2,1,0:T(2,128)S(1)}, f32[4,2,256]{2,1,0:T(2,128)}, u32[]{:S(2)}) %copy-start) | copy-done | bytes 8216
  2.1 53.9 %shard_map.146 = (bf16[64,512]{1,0:T(8,128)(2,1)S(1)}, f32[64,512]{1,0:T(8,128)S(1)}, f32[3,8,256]{2,1,0:T(8,128)S(1)}, f32[4,8]{1,0:T(4,128)S(1)}, f32[8,256]{1,0:T(8,128)S(1)}) custom-call(f32[10,512]{1,0:T(8,128)S(1)} %convert_add_fusion.small_hbm, bf16[256,512]{1,0:T(8,128)(2,1)} %series_hbm.1, bf16[3,512,256]{2,1,0:T(8,128)(2,1)} %bitcast.10, ...), custom_call_target="tpu_custom_call" | custom-call | tf_op jit(solution)/shard_map/pallas_call | solution.py:749
  56.0 0.7 %shard_map.147 = (bf16[64,512]{1,0:T(8,128)(2,1)}, f32[64,512]{1,0:T(8,128)}, f32[3,8,256]{2,1,0:T(8,128)}, f32[4,8]{1,0:T(4,128)}, f32[8,256]{1,0:T(8,128)}) custom-call(bf16[64,512]{1,0:T(8,128)(2,1)S(1)} %get-tuple-element.15.refs_0_, f32[64,512]{1,0:T(8,128)S(1)} %get-tuple-element.16.refs_1_, f32[3,8,256]{2,1,0:T(8,128)S(1)} %get-tuple-element.17.refs_2_, ...), custom_call_target="tpu_custom_call" | custom-call | tf_op jit(solution)/shard_map/pallas_call | solution.py:808
  (1 shorter events, 0.0 us)
Async XLA Ops:
  0.6 0.7 %copy-start.5 = (f32[4]{0:T(128)S(1)}, f32[4]{0:T(128)}, u32[]{:S(2)}) copy-start(f32[4]{0:T(128)} %param.15) | copy-start | bytes 52
  0.6 0.7 %copy-start.6 = (f32[4]{0:T(128)S(1)}, f32[4]{0:T(128)}, u32[]{:S(2)}) copy-start(f32[4]{0:T(128)} %param.14) | copy-start | bytes 52
  0.7 0.7 %copy-start.1 = (bf16[512,4]{0,1:T(4,128)(2,1)S(1)}, bf16[512,4]{0,1:T(4,128)(2,1)}, u32[]{:S(2)}) copy-start(bf16[512,4]{0,1:T(4,128)(2,1)} %param.13) | copy-start | bytes 12292
  0.7 0.7 %copy-start.2 = (f32[2,256]{1,0:T(2,128)S(1)}, f32[2,256]{1,0:T(2,128)}, u32[]{:S(2)}) copy-start(f32[2,256]{1,0:T(2,128)} %param.17) | copy-start | bytes 6148
  0.7 0.7 %copy-start.3 = (f32[256]{0:T(256)S(1)}, f32[256]{0:T(256)}, u32[]{:S(2)}) copy-start(f32[256]{0:T(256)} %param.19) | copy-start | bytes 3076
  0.7 0.7 %copy-start.4 = (f32[4]{0:T(128)S(1)}, f32[4]{0:T(128)}, u32[]{:S(2)}) copy-start(f32[4]{0:T(128)} %param.18) | copy-start | bytes 52
  1.4 0.7 %copy-start = (f32[4,2,256]{2,1,0:T(2,128)S(1)}, f32[4,2,256]{2,1,0:T(2,128)}, u32[]{:S(2)}) copy-start(f32[4,2,256]{2,1,0:T(2,128)} %param.16) | copy-start | bytes 24580

commit v7 on v6

--- a/solution.py
+++ b/solution.py
@@ -453,8 +453,12 @@
         totals = totals + norm_all[p]
     inv_row = lax.rsqrt(totals[0:1] / E + EPS)
     coef_row = inv_row * inv_row * inv_row * totals[1:2] / E
-    inv = jnp.broadcast_to(inv_row, (inner, rows)).T
-    coef = jnp.broadcast_to(coef_row, (inner, rows)).T
+
+    def down(row):
+        lanes = jnp.broadcast_to(row, (N, rows)).T
+        return jnp.concatenate([lanes] * (inner // N), axis=1)
+
+    inv, coef = down(inv_row), down(coef_row)
     grad_gated = inv * gain_grad - gated * coef
     grad_y = grad_gated * gate_act
     gy = bf(grad_y)
@@ -509,9 +513,11 @@
         core_stage(core1_send, core1_in, CORE1)
         along_y = mm_right(grad_y * ssm, pick, 1, 0, 2)
         final = jnp.exp(run_t[:, rows - 1 : rows]) * start.astype(F32) + own_keep[...]
-        return grad_b, grad_gate, grad_pre_c, along_y, softplus(shift_n), sigmoid(shift_n), final
-
-    grad_b, grad_gate, grad_pre_c, along_y, step_n, slope_n, final = exchange(
+        base = skip_wide * grad_y + step * inside_buf[...]
+        sizes = softplus(shift_n), sigmoid(shift_n)
+        return grad_b, grad_gate, grad_pre_c, along_y, *sizes, final, base, bf(weight * xw)
+
+    grad_b, grad_gate, grad_pre_c, along_y, step_n, slope_n, final, base, weighed = exchange(
         mm(grown, c, 0, 0),
         back_send,
         back_all,
@@ -525,9 +531,9 @@
     y_stage(core1_send, core1_in, y1_send, y1_all, ALONG_Y1, CORE1)
     after = collect(suffix_all, BACK2)
 
-    back_b = inside_buf[...] + remain * mm(b, after, 1, 1)
-    grad_x = skip_wide * grad_y + step * back_b
-    grad_b = grad_b + mm(weight * xw, after)
+    reached = mm(b, after, 1, 1)
+    grad_x = base + weight * reached
+    grad_b = grad_b + mm(weighed, after)
     gc = jnp.concatenate([grad_x, grad_b], axis=1) * conv_buf[:, xb_lanes]
     rim2_send[...] = gc[0:8]
     push(rim2_send, rim2_in, RIM2, (prv, mine))
@@ -548,7 +554,7 @@
     by_chip(mm(series[...], pre_own, 0, 0) + mm(rim_in[...], before, 0, 0), core2_send, slice(None))
     core_stage(core2_send, core2_in, CORE2)
 
-    x_back = mm_right(xw * back_b, pick, 1, 0, 2)
+    x_back = mm_right(xw * (inside_buf[...] + remain * reached), pick, 1, 0, 2)
     grad_cum = along_y - step_n * x_back
     carried = jnp.sum(
         jnp.where(choose, jnp.sum(after.astype(F32) * final, axis=1, keepdims=True), 0.0),

time: 56.9 us -> 56.7 us (level)
  no operation moved by 1% of the time
where the time goes in v7:
time: 56.7 us; the launch traced here: 56.5 us
  Pallas kernels  54.4 us (96%)
  local copies, waits for them, and re-layouts  1.37 us (2%)
  between operations  0.7 us (1%)
    pallas_call x1, Pallas kernels, body(): pl.pallas_call(functools.partial(kernel, n_tm, n_head), out_shape=out_sha...  53.7 us
    unnamed x14, local copies, waits for them, and re-layouts  1.37 us

profile of v7, /device:TPU:1, one launch (start us, length us, event | category | flops | bytes accessed | tf_op | source)
XLA Modules:
  0.0 56.5 jit_solution(4765373243748797978)
XLA Ops:
  0.6 0.0 copy-start.5
  0.6 0.0 copy-start.6
  0.7 0.0 copy-start.1
  0.7 0.0 copy-start.2
  0.7 0.0 copy-start.3
  0.7 0.0 copy-start.4
  0.7 0.6 %copy-done.5 = f32[4]{0:T(128)S(1)} copy-done((f32[4]{0:T(128)S(1)}, f32[4]{0:T(128)}, u32[]{:S(2)}) %copy-start.5) | copy-done | bytes 40
  1.3 0.0 copy-done.6
  1.3 0.0 copy-done.1
  1.4 0.0 copy-done.2
  1.4 0.0 copy-done.3
  1.4 0.0 copy-done.4
  1.4 0.0 copy-start
  1.4 0.7 %copy-done = f32[4,2,256]{2,1,0:T(2,128)S(1)} copy-done((f32[4,2,256]{2,1,0:T(2,128)S(1)}, f32[4,2,256]{2,1,0:T(2,128)}, u32[]{:S(2)}) %copy-start) | copy-done | bytes 8216
  2.1 53.7 %shard_map.146 = (bf16[64,512]{1,0:T(8,128)(2,1)S(1)}, f32[64,512]{1,0:T(8,128)S(1)}, f32[3,8,256]{2,1,0:T(8,128)S(1)}, f32[4,8]{1,0:T(4,128)S(1)}, f32[8,256]{1,0:T(8,128)S(1)}) custom-call(f32[10,512]{1,0:T(8,128)S(1)} %convert_add_fusion.small_hbm, bf16[256,512]{1,0:T(8,128)(2,1)} %series_hbm.1, bf16[3,512,256]{2,1,0:T(8,128)(2,1)} %bitcast.10, ...), custom_call_target="tpu_custom_call" | custom-call | tf_op jit(solution)/shard_map/pallas_call | solution.py:755
  55.8 0.7 %shard_map.147 = (bf16[64,512]{1,0:T(8,128)(2,1)}, f32[64,512]{1,0:T(8,128)}, f32[3,8,256]{2,1,0:T(8,128)}, f32[4,8]{1,0:T(4,128)}, f32[8,256]{1,0:T(8,128)}) custom-call(bf16[64,512]{1,0:T(8,128)(2,1)S(1)} %get-tuple-element.15.refs_0_, f32[64,512]{1,0:T(8,128)S(1)} %get-tuple-element.16.refs_1_, f32[3,8,256]{2,1,0:T(8,128)S(1)} %get-tuple-element.17.refs_2_, ...), custom_call_target="tpu_custom_call" | custom-call | tf_op jit(solution)/shard_map/pallas_call | solution.py:814
  (1 shorter events, 0.0 us)
Async XLA Ops:
  0.6 0.7 %copy-start.5 = (f32[4]{0:T(128)S(1)}, f32[4]{0:T(128)}, u32[]{:S(2)}) copy-start(f32[4]{0:T(128)} %param.15) | copy-start | bytes 52
  0.6 0.7 %copy-start.6 = (f32[4]{0:T(128)S(1)}, f32[4]{0:T(128)}, u32[]{:S(2)}) copy-start(f32[4]{0:T(128)} %param.14) | copy-start | bytes 52
  0.7 0.7 %copy-start.1 = (bf16[512,4]{0,1:T(4,128)(2,1)S(1)}, bf16[512,4]{0,1:T(4,128)(2,1)}, u32[]{:S(2)}) copy-start(bf16[512,4]{0,1:T(4,128)(2,1)} %param.13) | copy-start | bytes 12292
  0.7 0.7 %copy-start.2 = (f32[2,256]{1,0:T(2,128)S(1)}, f32[2,256]{1,0:T(2,128)}, u32[]{:S(2)}) copy-start(f32[2,256]{1,0:T(2,128)} %param.17) | copy-start | bytes 6148
  0.7 0.7 %copy-start.3 = (f32[256]{0:T(256)S(1)}, f32[256]{0:T(256)}, u32[]{:S(2)}) copy-start(f32[256]{0:T(256)} %param.19) | copy-start | bytes 3076
  0.7 0.7 %copy-start.4 = (f32[4]{0:T(128)S(1)}, f32[4]{0:T(128)}, u32[]{:S(2)}) copy-start(f32[4]{0:T(128)} %param.18) | copy-start | bytes 52
  1.4 0.7 %copy-start = (f32[4,2,256]{2,1,0:T(2,128)S(1)}, f32[4,2,256]{2,1,0:T(2,128)}, u32[]{:S(2)}) copy-start(f32[4,2,256]{2,1,0:T(2,128)} %param.16) | copy-start | bytes 24580
